TPU v7x, 32 devices: a whole 2x2x4 slice. The times are simulated.
32 devices in a mesh: pos: 8 (over z, core), trk: 4 (over y, x).
Axes of the slice: x: 2, y: 2, z: 4, core: 2. Of those that a mesh axis runs over, the one named last changes fastest.
Arguments:
- activations: bfloat16 [4, 4096, 1536], P(None, 'pos', 'trk'), may hold values from -6 to 6
- norm_gain: float32 [1536], P('trk'), may hold values from 0.1 to 1.9
- norm_bias: float32 [1536], P('trk'), may hold values from -1 to 1
- conv_weight: bfloat16 [3, 1536, 1536], P(None, None, 'trk'), may hold values from -0.09375 to 0.09375
- head_weight: bfloat16 [1536, 4096], P(None, 'trk'), may hold values from -0.15625 to 0.15625
- head_bias: float32 [4096], P('trk'), may hold values from -2 to 0
- gene_slot: int32 [4, 4096], P(None, 'pos'), may hold values from -1 to 35, as said below
- straddle_map: int32 [32], P('pos'), may hold values from -1 to 31, as said below
Outputs:
- tracks: bfloat16 [4, 4096, 4096], P(None, 'pos', 'trk')
- gene_mean: float32 [256, 4096], P('pos', 'trk')
Inputs may be any that keep to these rules, and one draw needn't show every extreme that they name: `gene_slot`: -1 marks a bin outside exons. A value g below 32 names gene g of the bin's own block of 512 positions; 32 + s names entry s of the previous block's straddle list and appears only where that entry is not -1, never in the first block. `straddle_map`: entry index * 4 + s names the gene of block index that entry s of its straddle list stands for, or -1; the live entries of one block are distinct, and the last block's are all -1.
All inputs are finite; a program needn't handle non-finite values.
Results may differ from a plain program's by a relative error of at most 0.0048.
Values may be sent and summed in bfloat16 or wider, within the bound.
No kernel may reach another device: no remote copies, remote signals or barrier semaphores. Data moves between devices by JAX's collectives and lax.ppermute only.
A program may use at most 128 MiB of HBM per device.

v0:
```python
import jax
import jax.numpy as jnp
from jax import lax
from jax.sharding import PartitionSpec as P

GENES_DEV = 32


def with_halo(cells, sides, width):
    for axis, dim in sides:
        count = lax.axis_size(axis)
        ends = count - 1
        head = lax.slice_in_dim(cells, 0, width, axis=dim)
        tail = lax.slice_in_dim(cells, cells.shape[dim] - width, cells.shape[dim], axis=dim)
        cells = jnp.concatenate(
            [
                lax.ppermute(tail, axis, [(i, (i + 1) % count) for i in range(ends)]),
                cells,
                lax.ppermute(head, axis, [((i + 1) % count, i) for i in range(ends)]),
            ],
            axis=dim,
        )
    return cells


def passed_along(value, axis, steps):
    count = lax.axis_size(axis)
    initial, last = (max(0, -steps), min(count, count - steps))
    return lax.ppermute(value, axis, [(source, source + steps) for source in range(initial, last)])


def per_device(
    activations, norm_gain, norm_bias, conv_weight, head_weight, head_bias, gene_slot, straddle_map
):
    sequences, length, channels = activations.shape
    total_rows = sequences * length
    hidden = jax.nn.gelu(
        activations.astype(jnp.float32) * norm_gain + norm_bias, approximate=True
    ).astype(jnp.bfloat16)
    zeros_init = jnp.zeros((total_rows, conv_weight.shape[2]), jnp.float32)
    gathered = lax.all_gather(hidden, "trk", axis=2, tiled=True)
    padded = with_halo(gathered, (("pos", 1),), 1)
    running = zeros_init
    columns = padded.shape[2]
    for tap_index in range(3):
        tap_rows = conv_weight[tap_index]
        window = padded[:, tap_index : tap_index + length, :].reshape(total_rows, columns)
        running = running + jnp.dot(window, tap_rows, preferred_element_type=jnp.float32)
    mixed = (activations.reshape(total_rows, channels).astype(jnp.float32) + running).astype(
        jnp.bfloat16
    )
    whole_mixed = lax.all_gather(mixed, "trk", axis=1, tiled=True)
    logits = jnp.dot(whole_mixed, head_weight, preferred_element_type=jnp.float32)
    tracks = jax.nn.softplus(logits + head_bias).astype(jnp.bfloat16)
    stride = straddle_map.shape[0]
    slot_ids = gene_slot.reshape(-1)
    onehot = (slot_ids[None, :] == jnp.arange(GENES_DEV + stride, dtype=jnp.int32)[:, None]).astype(
        jnp.bfloat16
    )
    slot_sums = jnp.dot(onehot, tracks, preferred_element_type=jnp.float32)
    counts = jnp.sum(onehot.astype(jnp.float32), axis=1)
    received, received_counts = passed_along((slot_sums[GENES_DEV:], counts[GENES_DEV:]), "pos", -1)
    owners = (straddle_map[:, None] == jnp.arange(GENES_DEV, dtype=jnp.int32)[None, :]).astype(
        jnp.float32
    )
    totals = slot_sums[:GENES_DEV] + jnp.dot(owners.T, received, precision=lax.Precision.HIGHEST)
    gene_counts = counts[:GENES_DEV] + jnp.dot(
        owners.T, received_counts, precision=lax.Precision.HIGHEST
    )
    gene_mean = totals / jnp.maximum(gene_counts, 1.0)[:, None]
    return (tracks.reshape(sequences, length, -1), gene_mean)


def solution(mesh):
    in_specs = (
        P(None, "pos", "trk"),
        P("trk"),
        P("trk"),
        P(None, None, "trk"),
        P(None, "trk"),
        P("trk"),
        P(None, "pos"),
        P("pos"),
    )
    out_specs = (P(None, "pos", "trk"), P("pos", "trk"))
    return jax.shard_map(
        per_device, mesh=mesh, in_specs=in_specs, out_specs=out_specs, check_vma=False
    )
```

profile of v0, /device:TPU:1, one launch (start us, length us, event | category | flops | bytes accessed | tf_op | source)
XLA Modules:
  0.0 203.5 jit_solution(5237592931833775700)
XLA Ops:
  7.2 0.0 copy-start
  7.2 0.0 all-gather.3.cloned.1.call-start
  7.2 4.0 %fusion.8 = bf16[4,512,384]{2,1,0:T(8,128)(2,1)} fusion(f32[384]{0:T(512)} %param.10, f32[384]{0:T(512)} %param.9, bf16[4,512,384]{2,1,0:T(8,128)(2,1)} %param.8), kind=kLoop, calls=%fused_computation.12 | loop fusion | flops 9437184 | bytes 3148800 | tf_op jit(solution)/shard_map/convert_element_type | solution.py:39
  11.3 0.0 all-gather.3.cloned.1.call-update
  11.3 0.0 all-gather.5.cloned.1.call-start
  11.3 71.9 %all-gather.3.cloned.1.call-done = bf16[4,512,1536]{2,1,0:T(8,128)(2,1)} async-done(((bf16[4,512,384]{2,1,0:T(8,128)(2,1)}), bf16[4,512,1536]{2,1,0:T(8,128)(2,1)}) %all-gather.3.cloned.1.call-update) | async-done | bytes 6291472 | tf_op jit(solution)/shard_map/all_gather | solution.py:41
  83.2 1.0 fusion.30
  84.2 3.8 %collective-permute-start = (bf16[4,1,1536]{2,1,0:T(2,128)(2,1)S(1)}, bf16[4,1,1536]{2,1,0:T(2,128)(2,1)S(1)}, u32[]{:S(2)}, u32[]{:S(2)}) collective-permute-start(bf16[4,1,1536]{2,1,0:T(2,128)(2,1)S(1)} %get-tuple-element.5), channel_id=1, source_target_pairs={{0,4},{4,8},{8,12},{12,16},{16,20},{20,24},{24,28},{1,5},{5,9},{9,... | collective-permute-start | bytes 36872 | tf_op jit(solution)/shard_map/ppermute | solution.py:17
  88.1 1.9 collective-permute-start.1
  90.0 0.0 slice-start
  90.0 0.0 slice-start.1
  90.0 6.0 %fusion.14 = f32[2048,384]{1,0:T(8,128)S(1)} fusion(bf16[2048,1536]{1,0:T(8,128)(2,1)} %bitcast.37, bf16[3,1536,384]{2,1,0:T(8,128)(2,1)} %param.11), kind=kOutput, calls=%fused_computation.17 | convolution fusion | flops 2415919104 | bytes 10616832 | tf_op jit(solution)/shard_map/dot_general | solution.py:48
  96.0 0.0 copy-start.4
  96.0 0.0 collective-permute-done
  96.0 0.0 collective-permute-done.1
  96.0 0.0 slice-done
  96.0 0.0 slice-done.1
  96.0 3.4 %pad_maximum_fusion = (bf16[4,512,1536]{2,1,0:T(8,128)(2,1)S(1)}, bf16[4,512,1536]{2,1,0:T(8,128)(2,1)S(1)}) fusion(bf16[4,1,1536]{2,1,0:T(2,128)(2,1)S(1)} %collective-permute-done.1, bf16[4,512,1536]{2,1,0:T(8,128)(2,1)S(1)} %bitcast.39, bf16[4,1,1536]{2,1,0:T(2,128)(2,1)S(1)} %collective-permute-done), kind=kLoop, calls=%fused_computation.2 | loop fusion | flops 25165824 | bytes 18898944 | tf_op jit(solution)/shard_map/concatenate | solution.py:15
  99.4 0.0 copy-done.4
  99.4 0.0 copy-start.2
  99.5 3.4 %fusion.16 = f32[2048,384]{1,0:T(8,128)S(1)} fusion(bf16[2048,1536]{1,0:T(8,128)(2,1)S(1)} %bitcast.41, bf16[3,1536,384]{2,1,0:T(8,128)(2,1)S(1)} %copy-done.4), kind=kOutput, calls=%fused_computation.19 | convolution fusion | flops 2415919104 | bytes 10616832 | tf_op jit(solution)/shard_map/dot_general | solution.py:48
  102.9 0.0 copy-done.2
  102.9 0.0 copy-start.3
  102.9 0.0 copy-start.5
  102.9 4.5 %fusion.9 = bf16[2048,384]{1,0:T(8,128)(2,1)} fusion(f32[2048,384]{1,0:T(8,128)S(1)} %fusion.16, f32[2048,384]{1,0:T(8,128)S(1)} %fusion.14, bf16[2048,1536]{1,0:T(8,128)(2,1)S(1)} %bitcast.40, bf16[3,1536,384]{2,1,0:T(8,128)(2,1)S(1)} %copy-done.4, bf16[4,512,384]{2,1,0:T(8,128)(2,1)S(1)} %copy-done.2), kind=kOutput, calls=%fused_computation.14 | convolution fusion | flops 2419851264 | bytes 16908288 | tf_op jit(solution)/shard_map/dot_general | solution.py:48
  107.5 0.0 all-gather.5.cloned.1.call-update
  107.5 0.0 copy-done.3
  107.5 0.1 convert_reduce_fusion
  107.7 0.1 slice.45
  107.7 2.1 %collective-permute-start.3 = (f32[4]{0:T(128)S(1)}, f32[4]{0:T(128)S(1)}, u32[]{:S(2)}, u32[]{:S(2)}) collective-permute-start(f32[4]{0:T(128)S(1)} %slice.45), channel_id=1, source_target_pairs={{4,0},{8,4},{12,8},{16,12},{20,16},{24,20},{28,24},{5,1},{9,5},{13... | collective-permute-start | bytes 56 | tf_op jit(solution)/shard_map/ppermute | solution.py:29
  109.8 67.5 %all-gather.5.cloned.1.call-done = bf16[2048,1536]{1,0:T(8,128)(2,1)} async-done(((bf16[2048,384]{1,0:T(8,128)(2,1)}), bf16[2048,1536]{1,0:T(8,128)(2,1)}) %all-gather.5.cloned.1.call-update) | async-done | bytes 6291472 | tf_op jit(solution)/shard_map/all_gather | solution.py:52
  177.4 0.0 copy-done
  177.4 0.0 copy-done.5
  177.4 12.2 %fusion = bf16[2048,1024]{1,0:T(8,128)(2,1)S(1)} fusion(f32[1024]{0:T(1024)S(1)} %copy-done.5, bf16[2048,1536]{1,0:T(8,128)(2,1)} %all-gather.5.cloned.1.call-done, bf16[1536,1024]{1,0:T(8,128)(2,1)S(1)} %copy-done), kind=kOutput, calls=%fused_computation.1 | convolution fusion | flops 6459228160 | bytes 13635584 | tf_op jit(solution)/shard_map/dot_general | solution.py:53
  189.6 0.0 copy-start.1
  189.6 0.0 copy-start.6
  189.6 0.8 fusion.25
  190.4 2.8 %collective-permute-start.2 = (f32[4,1024]{1,0:T(4,128)S(1)}, f32[4,1024]{1,0:T(4,128)S(1)}, u32[]{:S(2)}, u32[]{:S(2)}) collective-permute-start(f32[4,1024]{1,0:T(4,128)S(1)} %slice.49), channel_id=1, source_target_pairs={{4,0},{8,4},{12,8},{16,12},{20,16},{24,20},{28,24},{5,1},{9,5},{13... | collective-permute-start | bytes 49160 | tf_op jit(solution)/shard_map/ppermute | solution.py:29
  193.2 0.0 collective-permute-done.3
  193.2 0.0 copy-done.6
  193.2 0.1 fusion.23
  193.3 2.4 %collective-permute-done.2 = f32[4,1024]{1,0:T(4,128)S(1)} collective-permute-done((f32[4,1024]{1,0:T(4,128)S(1)}, f32[4,1024]{1,0:T(4,128)S(1)}, u32[]{:S(2)}, u32[]{:S(2)}) %collective-permute-start.2) | collective-permute-done | bytes 16416 | tf_op jit(solution)/shard_map/ppermute | solution.py:29
  195.7 1.0 fusion.21
  196.7 0.0 copy-done.1
  (3 shorter events, 0.0 us)
Async XLA Ops:
  7.2 170.2 %copy-start = (bf16[1536,1024]{1,0:T(8,128)(2,1)S(1)}, bf16[1536,1024]{1,0:T(8,128)(2,1)}, u32[]{:S(2)}) copy-start(bf16[1536,1024]{1,0:T(8,128)(2,1)} %param.12) | copy-start | bytes 9437188
  7.2 76.1 %all-gather.3.cloned.1.call-start = ((), (), s32[]{:S(2)}) async-start(), calls=%async_computation | async-start | bytes 7864320 | tf_op jit(solution)/shard_map/all_gather | solution.py:41
  11.3 166.1 %all-gather.5.cloned.1.call-start = ((), (), s32[]{:S(2)}) async-start(), calls=%async_computation.1 | async-start | bytes 7864320 | tf_op jit(solution)/shard_map/all_gather | solution.py:52
  84.2 11.8 %collective-permute-start = (bf16[4,1,1536]{2,1,0:T(2,128)(2,1)S(1)}, bf16[4,1,1536]{2,1,0:T(2,128)(2,1)S(1)}, u32[]{:S(2)}, u32[]{:S(2)}) collective-permute-start(bf16[4,1,1536]{2,1,0:T(2,128)(2,1)S(1)} %get-tuple-element.5), channel_id=1, source_target_pairs={{0,4},{4,8},{8,12},{12,16},{16,20},{20,24},{24,28},{1,5},{5,9},{9,... | collective-permute-start | bytes 36872 | tf_op jit(solution)/shard_map/ppermute | solution.py:17
  88.1 7.9 %collective-permute-start.1 = (bf16[4,1,1536]{2,1,0:T(2,128)(2,1)S(1)}, bf16[4,1,1536]{2,1,0:T(2,128)(2,1)S(1)}, u32[]{:S(2)}, u32[]{:S(2)}) collective-permute-start(bf16[4,1,1536]{2,1,0:T(2,128)(2,1)S(1)} %get-tuple-element.4), channel_id=1, source_target_pairs={{4,0},{8,4},{12,8},{16,12},{20,16},{24,20},{28,24},{5,1},{9,5},{13... | collective-permute-start | bytes 36872 | tf_op jit(solution)/shard_map/ppermute | solution.py:19
  90.0 6.0 %slice-start = ((s8[6291456]{0:T(1024)(128)(4,1)}), s8[4194304]{0:T(1024)(128)(4,1)S(1)}, s32[]{:S(2)}) async-start(s8[6291456]{0:T(1024)(128)(4,1)} %bitcast.38), calls=%async_computation.2 | async-start | bytes 8388608
  90.0 6.0 %slice-start.1 = ((s8[6291456]{0:T(1024)(128)(4,1)}), s8[2097152]{0:T(1024)(128)(4,1)S(1)}, s32[]{:S(2)}) async-start(s8[6291456]{0:T(1024)(128)(4,1)} %bitcast.38), calls=%async_computation.3 | async-start | bytes 4194304
  96.0 3.5 %copy-start.4 = (bf16[3,1536,384]{2,1,0:T(8,128)(2,1)S(1)}, bf16[3,1536,384]{2,1,0:T(8,128)(2,1)}, u32[]{:S(2)}) copy-start(bf16[3,1536,384]{2,1,0:T(8,128)(2,1)} %param.11) | copy-start | bytes 10616836
  99.4 3.5 %copy-start.2 = (bf16[4,512,384]{2,1,0:T(8,128)(2,1)S(1)}, bf16[4,512,384]{2,1,0:T(8,128)(2,1)}, u32[]{:S(2)}) copy-start(bf16[4,512,384]{2,1,0:T(8,128)(2,1)} %param.8) | copy-start | bytes 4718596
  102.9 4.6 %copy-start.3 = (s32[4,512]{1,0:T(4,128)S(1)}, s32[4,512]{1,0:T(4,128)}, u32[]{:S(2)}) copy-start(s32[4,512]{1,0:T(4,128)} %param.14) | copy-start | bytes 24580
  102.9 74.4 %copy-start.5 = (f32[1024]{0:T(1024)S(1)}, f32[1024]{0:T(1024)}, u32[]{:S(2)}) copy-start(f32[1024]{0:T(1024)} %param.13) | copy-start | bytes 12292
  107.7 85.5 %collective-permute-start.3 = (f32[4]{0:T(128)S(1)}, f32[4]{0:T(128)S(1)}, u32[]{:S(2)}, u32[]{:S(2)}) collective-permute-start(f32[4]{0:T(128)S(1)} %slice.45), channel_id=1, source_target_pairs={{4,0},{8,4},{12,8},{16,12},{20,16},{24,20},{28,24},{5,1},{9,5},{13... | collective-permute-start | bytes 56 | tf_op jit(solution)/shard_map/ppermute | solution.py:29
  189.6 7.1 %copy-start.1 = (bf16[2048,1024]{1,0:T(8,128)(2,1)}, bf16[2048,1024]{1,0:T(8,128)(2,1)S(1)}, u32[]{:S(2)}) copy-start(bf16[2048,1024]{1,0:T(8,128)(2,1)S(1)} %fusion) | copy-start | bytes 12582916
  189.6 3.6 %copy-start.6 = (s32[4]{0:T(128)S(1)}, s32[4]{0:T(128)}, u32[]{:S(2)}) copy-start(s32[4]{0:T(128)} %param.15) | copy-start | bytes 52
  190.4 5.3 %collective-permute-start.2 = (f32[4,1024]{1,0:T(4,128)S(1)}, f32[4,1024]{1,0:T(4,128)S(1)}, u32[]{:S(2)}, u32[]{:S(2)}) collective-permute-start(f32[4,1024]{1,0:T(4,128)S(1)} %slice.49), channel_id=1, source_target_pairs={{4,0},{8,4},{12,8},{16,12},{20,16},{24,20},{28,24},{5,1},{9,5},{13... | collective-permute-start | bytes 49160 | tf_op jit(solution)/shard_map/ppermute | solution.py:29
Sparse Core Ops, SparseCore 0:
  11.4 71.7 all-gather.2
  107.6 69.6 all-gather.4
where the time goes:
time: 204 us
  waiting for transfers between devices  142 us (70%)
  matrix products  28.1 us (14%)
  between operations  14.3 us (7%)
  starting transfers between devices  10.7 us (5%)
  other arithmetic  7.56 us (4%)
    all_gather x1, waiting for transfers between devices, per_device(): gathered = lax.all_gather(hidden, 'trk', axis=2, tiled=True)  71.9 us
    all_gather x1, waiting for transfers between devices, per_device(): whole_mixed = lax.all_gather(mixed, 'trk', axis=1, tiled=True)  67.5 us
    dot_general x3, matrix products, per_device(): jnp.dot(window, tap_rows, preferred_element_type=jnp.float32)  13.9 us
    dot_general x1, matrix products, per_device(): jnp.dot(whole_mixed, head_weight, preferred_element_type=jnp.float32)  12.2 us
    ppermute x2, starting transfers between devices, passed_along(): lax.ppermute(value, axis, [(source, source + steps) for source in range(i...  4.84 us
  transfers between devices with their start and end apart: 6, of which 3 were waited for; matrix products, arithmetic and copies ran while one was open for 10% of the time, Pallas kernels for 0%

commit v1 on v0

v1 whole, which is shorter than its diff:
```python
import functools

import jax
import jax.numpy as jnp
from jax import lax
from jax.experimental import pallas as pl
from jax.experimental.pallas import tpu as pltpu
from jax.sharding import PartitionSpec as P


GENES_DEV = 32
LANES = 128
LIMIT = 24 << 20
EDGE = 16
SIDE = 8
VMEM = pl.BlockSpec(memory_space=pltpu.VMEM)
ANY = pl.BlockSpec(memory_space=pl.ANY)
SMEM = pl.BlockSpec(memory_space=pltpu.SMEM)


def swap(value, bit):
    count = lax.axis_size("trk")
    return lax.ppermute(value, "trk", [(i, i ^ bit) for i in range(count)])


def split_bits(j):
    return j & -j, 1 << (j.bit_length() - 1)


def passed_along(value, axis, steps):
    count = lax.axis_size(axis)
    initial, last = (max(0, -steps), min(count, count - steps))
    return lax.ppermute(value, axis, [(source, source + steps) for source in range(initial, last)])


def spread(own, cut, rows):
    count = lax.axis_size("trk")
    wholes, parts = {0: own}, {}

    def piece(j, part):
        if j in wholes:
            return wholes[j][:cut] if part == 0 else wholes[j][cut:rows]
        return parts[j][part]

    places = [[(own, 0, cut), (own, cut, rows - cut)]]
    for j in range(1, count):
        low, high = split_bits(j)
        if low == high:
            wholes[j] = swap(own, j)
            places.append([(wholes[j], 0, cut), (wholes[j], cut, rows - cut)])
        else:
            parts[j] = (swap(piece(j ^ high, 0), high), swap(piece(j ^ low, 1), low))
            places.append([(parts[j][0], 0, cut), (parts[j][1], 0, rows - cut)])
    return places, wholes


def gelu_of(values, gain, bias):
    return jax.nn.gelu(values.astype(jnp.float32) * gain + bias, approximate=True)


def first_kernel(group, act_ref, all_ref, gain_ref, bias_ref, out_ref, tail_ref, head_ref, edges, sems):
    sequences, length, channels = all_ref.shape
    gain, bias = gain_ref[...][None], bias_ref[...][None]
    copies = []
    for s in range(sequences):
        for side, start in enumerate((length - EDGE, 0)):
            copies.append(
                pltpu.make_async_copy(
                    all_ref.at[s, pl.ds(start, EDGE)], edges.at[s, side], sems.at[s, side]
                )
            )
            copies[-1].start()
    for copy in copies:
        copy.wait()
    index = lax.broadcasted_iota(jnp.int32, (SIDE, channels), 0)
    tails = jnp.zeros((SIDE, channels), jnp.float32)
    heads = tails
    for s in range(sequences):
        tail = edges[s, 0].astype(jnp.float32)[EDGE - 1 :]
        head = edges[s, 1].astype(jnp.float32)[:1]
        tails = jnp.where(index == s, tail, tails)
        heads = jnp.where(index == s, head, heads)
    tail_ref[...] = gelu_of(tails, gain, bias).astype(jnp.bfloat16)
    head_ref[...] = gelu_of(heads, gain, bias).astype(jnp.bfloat16)
    for s in range(group):
        out_ref[s * length : (s + 1) * length, :] = gelu_of(act_ref[s], gain, bias).astype(jnp.bfloat16)


def second_kernel(act_ref, gain_ref, bias_ref, tail_ref, head_ref, out_ref):
    group, length, _ = act_ref.shape
    gain, bias = gain_ref[...][None], bias_ref[...][None]
    for s in range(group):
        out_ref[s * length : (s + 1) * length, :] = gelu_of(act_ref[s], gain, bias).astype(jnp.bfloat16)
    rows = group * length
    out_ref[rows : rows + EDGE, :] = jnp.concatenate(
        [tail_ref[...].astype(jnp.float32), head_ref[...].astype(jnp.float32)]
    ).astype(jnp.bfloat16)


def rows_of(plan, refs, start, size):
    out = []
    for places in plan:
        row, found = 0, []
        for which, first, extent in places:
            low, high = max(start, row), min(start + size, row + extent)
            if low < high:
                found.append(refs[which][first + low - row : first + high - row, :])
            row += extent
        out.append(found[0] if len(found) == 1 else jnp.concatenate(found))
    return jnp.concatenate(out, axis=1)


def conv_kernel(first, group, plan, edge_plan, n_blocks, t_ref, act_ref, w_ref, *refs):
    blocks, out_ref = refs[:n_blocks], refs[n_blocks]
    _, length, channels = act_ref.shape
    t = t_ref[0]
    count = len(plan)
    starts = [pl.multiple_of((t ^ j) * channels, channels) for j in range(count)]
    weight = jnp.concatenate(
        [jnp.concatenate([w_ref[k, pl.ds(start, channels), :] for start in starts]) for k in range(3)], axis=1
    )
    edge = jnp.concatenate([blocks[which][start : start + EDGE, :] for which, start in edge_plan], axis=1)
    row = lax.broadcasted_iota(jnp.int32, (length, channels), 0)
    for s in range(group):
        values = jnp.concatenate([rows_of(plan, blocks, s * length, length), edge])
        made = jnp.dot(values, weight, preferred_element_type=jnp.float32)
        before, at, after = (made[:, k * channels : (k + 1) * channels] for k in range(3))
        place = length + first + s
        left = jnp.where(row == 0, before[place : place + 1], pltpu.roll(before[:length], 1, 0))
        place += SIDE
        right = jnp.where(
            row == length - 1, after[place : place + 1], pltpu.roll(after[:length], length - 1, 0)
        )
        total = act_ref[s].astype(jnp.float32) + ((left + at[:length]) + right)
        out_ref[s * length : (s + 1) * length, :] = total.astype(jnp.bfloat16)


def head_kernel(first, group, length, plan, n_blocks, last, t_ref, w_ref, bias_ref, slot_ref, *refs):
    blocks = refs[:n_blocks]
    refs = refs[n_blocks:]
    if last:
        own_in, strad_in, _ = refs[:3]
        refs = refs[3:]
    tracks_ref, own_ref, strad_ref, made, out_sems = refs
    t = t_ref[0]
    count = len(plan)
    channels = w_ref.shape[0] // count
    starts = [pl.multiple_of((t ^ j) * channels, channels) for j in range(count)]
    weight = jnp.concatenate([w_ref[pl.ds(start, channels), :] for start in starts])
    n_own, n_strad = own_ref.shape[0], strad_ref.shape[0]
    index = lax.broadcasted_iota(jnp.int32, (n_own + n_strad, length), 0)
    if last:
        sums = jnp.concatenate([own_in[...], strad_in[...]])
    else:
        sums = jnp.zeros((n_own + n_strad, w_ref.shape[1]), jnp.float32)
    bias = bias_ref[...][None]
    outs = []
    for s in range(group):
        logits = jnp.dot(rows_of(plan, blocks, s * length, length), weight, preferred_element_type=jnp.float32)
        logits = logits + bias
        part = jnp.maximum(logits, 0.0) + jnp.log1p(jnp.exp(-jnp.abs(logits)))
        made[s] = part.astype(jnp.bfloat16)
        outs.append(pltpu.make_async_copy(made.at[s], tracks_ref.at[first + s], out_sems.at[s]))
        outs[-1].start()
        onehot = (index == slot_ref[first + s : first + s + 1, :]).astype(jnp.bfloat16)
        sums = sums + jnp.dot(onehot, made[s], preferred_element_type=jnp.float32)
    own_ref[...] = sums[:n_own]
    strad_ref[...] = sums[n_own:]
    for copy in outs:
        copy.wait()


def arrays_of(places):
    arrays, plan = [], []

    def index(array):
        for i, other in enumerate(arrays):
            if other is array:
                return i
        arrays.append(array)
        return len(arrays) - 1

    for block in places:
        plan.append([(index(array), start, size) for array, start, size in block])
    return arrays, plan, index


def cost(flops, nbytes, calls=0):
    return pl.CostEstimate(flops=int(flops), bytes_accessed=int(nbytes), transcendentals=int(calls))


def by_kernels(
    activations, norm_gain, norm_bias, conv_weight, head_weight, head_bias, gene_slot, straddle_map
):
    sequences, length, channels = activations.shape
    count = lax.axis_size("trk")
    t = lax.axis_index("trk").astype(jnp.int32)[None]
    whole = channels * count
    n_tracks = head_weight.shape[1]
    group = sequences // 2
    rows = group * length
    cut = (group // 2) * length
    bf16, f32 = jnp.bfloat16, jnp.float32

    edge_shape = jax.ShapeDtypeStruct((SIDE, channels), bf16)
    first, tails, heads = pl.pallas_call(
        functools.partial(first_kernel, group),
        out_shape=(jax.ShapeDtypeStruct((rows, channels), bf16), edge_shape, edge_shape),
        grid=(1,),
        in_specs=[pl.BlockSpec((group, length, channels), lambda i: (0, 0, 0)), ANY, VMEM, VMEM],
        out_specs=(VMEM,) * 3,
        scratch_shapes=[pltpu.VMEM((sequences, 2, EDGE, channels), bf16), pltpu.SemaphoreType.DMA((sequences, 2))],
        compiler_params=pltpu.CompilerParams(vmem_limit_bytes=LIMIT),
        cost_estimate=cost(rows * channels * 20, rows * channels * 6, rows * channels),
    )(activations, activations, norm_gain, norm_bias)
    before, after = passed_along(tails, "pos", 1), passed_along(heads, "pos", -1)
    second = pl.pallas_call(
        second_kernel,
        out_shape=jax.ShapeDtypeStruct((rows + EDGE, channels), bf16),
        grid=(1,),
        in_specs=[pl.BlockSpec((group, length, channels), lambda i: (1, 0, 0))] + [VMEM] * 4,
        out_specs=VMEM,
        compiler_params=pltpu.CompilerParams(vmem_limit_bytes=LIMIT),
        cost_estimate=cost(rows * channels * 20, rows * channels * 6, rows * channels),
    )(activations, norm_gain, norm_bias, before, after)
    first_places, _ = spread(first, cut, rows)
    second_places, wholes = spread(second, cut, rows)
    edges = {j: (array, rows) for j, array in wholes.items()}
    for j in range(1, count):
        low, high = split_bits(j)
        if low != high:
            array, start = edges[j ^ high]
            edges[j] = (swap(array[start : start + EDGE], high), 0)

    def conv(i, places):
        arrays, plan, index = arrays_of(places)
        edge_plan = [(index(edges[j][0]), edges[j][1]) for j in range(count)]
        return pl.pallas_call(
            functools.partial(conv_kernel, i * group, group, plan, edge_plan, len(arrays)),
            out_shape=jax.ShapeDtypeStruct((rows, channels), bf16),
            grid=(1,),
            in_specs=[SMEM, pl.BlockSpec((group, length, channels), lambda _: (i, 0, 0))]
            + [VMEM] * (1 + len(arrays)),
            out_specs=VMEM,
            compiler_params=pltpu.CompilerParams(vmem_limit_bytes=LIMIT),
            cost_estimate=cost(6 * rows * whole * channels, 2 * rows * whole + 6 * whole * channels),
        )(t, activations, conv_weight, *arrays)

    mixed = [spread(conv(i, places), cut, rows)[0] for i, places in enumerate((first_places, second_places))]

    stride = straddle_map.shape[0]
    n_strad = -(-stride // 8) * 8
    sums = ()
    tracks = None
    for i in range(2):
        arrays, plan, _ = arrays_of(mixed[i])
        extra = () if i == 0 else (*sums, tracks)
        tracks, *sums = pl.pallas_call(
            functools.partial(head_kernel, i * group, group, length, plan, len(arrays), i == 1),
            out_shape=(
                jax.ShapeDtypeStruct((sequences, length, n_tracks), bf16),
                jax.ShapeDtypeStruct((GENES_DEV, n_tracks), f32),
                jax.ShapeDtypeStruct((n_strad, n_tracks), f32),
            ),
            in_specs=[SMEM, VMEM, VMEM, VMEM] + [VMEM] * len(arrays) + ([VMEM, VMEM, ANY] if i else []),
            out_specs=(ANY, VMEM, VMEM),
            input_output_aliases={4 + len(arrays) + 2: 0} if i else {},
            scratch_shapes=[
                pltpu.VMEM((group, length, n_tracks), bf16),
                pltpu.SemaphoreType.DMA((group,)),
            ],
            compiler_params=pltpu.CompilerParams(vmem_limit_bytes=LIMIT),
            cost_estimate=cost(
                2 * rows * whole * n_tracks,
                2 * rows * (whole + n_tracks) + 2 * whole * n_tracks,
                2 * rows * n_tracks,
            ),
        )(t, head_weight, head_bias, gene_slot, *arrays, *extra)
    return tracks, gene_mean_of(*sums, gene_slot, straddle_map)


def by_ops(
    activations, norm_gain, norm_bias, conv_weight, head_weight, head_bias, gene_slot, straddle_map
):
    sequences, length, channels = activations.shape
    rows = sequences * length
    f32, bf16 = jnp.float32, jnp.bfloat16
    hidden = gelu_of(activations, norm_gain, norm_bias).astype(bf16)
    gathered = lax.all_gather(hidden, "trk", axis=2, tiled=True)
    padded = jnp.concatenate(
        [passed_along(gathered[:, -1:], "pos", 1), gathered, passed_along(gathered[:, :1], "pos", -1)], axis=1
    )
    total = jnp.zeros((rows, conv_weight.shape[2]), f32)
    for k in range(3):
        window = padded[:, k : k + length].reshape(rows, -1)
        total = total + jnp.dot(window, conv_weight[k], preferred_element_type=f32)
    mixed = (activations.reshape(rows, channels).astype(f32) + total).astype(bf16)
    mixed = lax.all_gather(mixed, "trk", axis=1, tiled=True)
    logits = jnp.dot(mixed, head_weight, preferred_element_type=f32)
    tracks = jax.nn.softplus(logits + head_bias).astype(bf16)
    slots = jnp.arange(GENES_DEV + straddle_map.shape[0], dtype=jnp.int32)
    onehot = (gene_slot.reshape(-1)[None, :] == slots[:, None]).astype(bf16)
    sums = jnp.dot(onehot, tracks, preferred_element_type=f32)
    mean = gene_mean_of(sums[:GENES_DEV], sums[GENES_DEV:], gene_slot, straddle_map)
    return tracks.reshape(sequences, length, -1), mean


def gene_mean_of(own, strad, gene_slot, straddle_map):
    stride = straddle_map.shape[0]
    f32 = jnp.float32
    slots = jnp.arange(GENES_DEV + stride, dtype=jnp.int32)
    counts = jnp.sum((gene_slot.reshape(-1)[None, :] == slots[:, None]).astype(f32), axis=1)
    received_counts = passed_along(counts[GENES_DEV:], "pos", -1)
    owners = (straddle_map[None, :] == jnp.arange(GENES_DEV, dtype=jnp.int32)[:, None]).astype(f32)
    gene_counts = counts[:GENES_DEV] + jnp.sum(owners * received_counts[None], axis=1)
    received = passed_along(strad, "pos", -1)[:stride]
    totals = own + jnp.dot(owners, received, precision=lax.Precision.HIGHEST)
    return totals / jnp.maximum(gene_counts, 1.0)[:, None]


def per_device(*args):
    lanes = args[0].shape[2] % LANES == 0 and args[4].shape[1] % LANES == 0
    return (by_kernels if lanes else by_ops)(*args)


def solution(mesh):
    in_specs = (
        P(None, "pos", "trk"),
        P("trk"),
        P("trk"),
        P(None, None, "trk"),
        P(None, "trk"),
        P("trk"),
        P(None, "pos"),
        P("pos"),
    )
    out_specs = (P(None, "pos", "trk"), P("pos", "trk"))
    return jax.shard_map(
        per_device, mesh=mesh, in_specs=in_specs, out_specs=out_specs, check_vma=False
    )
```

time: 204 us -> 137 us (0.67)
  waiting for transfers between devices: 142 us -> 62.7 us
  matrix products: 28.1 us -> 0.33 us
  Pallas kernels: 0 us -> 24.3 us
  starting transfers between devices: 10.7 us -> 33.9 us
  between operations: 14.3 us -> 0.85 us
  local copies, waits for them, and re-layouts: 1.12 us -> 13.8 us
  other arithmetic: 7.56 us -> 0.98 us
    all_gather x2 -> x0, waiting for transfers between devices: 139 us -> none  [the longest x1 71.9 us: per_device(): gathered = lax.all_gather(hidden, 'trk', axis=2, tiled=True)]
    ppermute x2 -> x17, waiting for transfers between devices: 0.01 us -> 56.7 us  [swap(): return lax.ppermute(value, 'trk', [(i, i ^ bit) for i in range(count)])]
    dot_general x7 -> x1, matrix products: 28.1 us -> 0.33 us  [gene_mean_of(): totals = own + jnp.dot(owners, received, precision=lax.Precision.HIGHEST)]
    pallas_call x0 -> x6, Pallas kernels: none -> 24.3 us  [the longest x2 11.7 us: by_kernels(): pl.pallas_call(functools.partial(head_kernel, i * group, group, length, p...]
    ppermute x2 -> x4, starting transfers between devices: 4.84 us -> 18.1 us  [passed_along(): lax.ppermute(value, axis, [(source, source + steps) for source in range(i...]
    unnamed x19 -> x37, local copies, waits for them, and re-layouts: 0.06 us -> 10.2 us
    ppermute x2 -> x17, starting transfers between devices: 5.76 us -> 15.8 us  [swap(): return lax.ppermute(value, 'trk', [(i, i ^ bit) for i in range(count)])]
    convert_element_type x1 -> x0, other arithmetic: 4.03 us -> none  [per_device(): hidden = jax.nn.gelu(activations.astype(jnp.float32) * norm_gain + norm_b...]
  transfers between devices with their start and end apart: 6 -> 21, of which waited for: 3 -> 10; matrix products, arithmetic and copies ran while one was open for 10% -> 3% of each run, Pallas kernels for 0% -> 13%
where the time goes in v1:
time: 137 us
  waiting for transfers between devices  62.7 us (46%)
  starting transfers between devices  33.9 us (25%)
  Pallas kernels  24.3 us (18%)
  local copies, waits for them, and re-layouts  13.8 us (10%)
    ppermute x17, waiting for transfers between devices, swap(): return lax.ppermute(value, 'trk', [(i, i ^ bit) for i in range(count)])  56.7 us
    ppermute x4, starting transfers between devices, passed_along(): lax.ppermute(value, axis, [(source, source + steps) for source in range(i...  18.1 us
    ppermute x17, starting transfers between devices, swap(): return lax.ppermute(value, 'trk', [(i, i ^ bit) for i in range(count)])  15.8 us
    pallas_call x2, Pallas kernels, by_kernels(): pl.pallas_call(functools.partial(head_kernel, i * group, group, length, p...  11.7 us
    pallas_call x2, Pallas kernels, conv(): pl.pallas_call(functools.partial(conv_kernel, i * group, group, plan, edg...  11.1 us
    unnamed x37, local copies, waits for them, and re-layouts  10.2 us
    ppermute x4, waiting for transfers between devices, passed_along(): lax.ppermute(value, axis, [(source, source + steps) for source in range(i...  5.96 us
    slice x8, local copies, waits for them, and re-layouts, piece(): return wholes[j][:cut] if part == 0 else wholes[j][cut:rows]  3.46 us
  transfers between devices with their start and end apart: 21, of which 10 were waited for; matrix products, arithmetic and copies ran while one was open for 3% of the time, Pallas kernels for 13%

profile of v1, /device:TPU:1, one launch (start us, length us, event | category | flops | bytes accessed | tf_op | source)
XLA Modules:
  0.0 136.8 jit_solution(2622509958484867356)
XLA Ops:
  0.6 0.0 copy-start
  0.6 1.4 %copy-done = bf16[4,512,384]{2,1,0:T(8,128)(2,1)S(1)} copy-done((bf16[4,512,384]{2,1,0:T(8,128)(2,1)S(1)}, bf16[4,512,384]{2,1,0:T(8,128)(2,1)}, u32[]{:S(2)}) %copy-start) | copy-done | bytes 1572888
  2.0 0.7 copy-done.9
  2.7 0.7 copy-done.10
  3.4 0.9 shard_map.95
  4.3 0.0 copy-start.1
  4.3 2.1 %collective-permute-start.11 = (bf16[1024,384]{1,0:T(8,128)(2,1)S(1)}, bf16[1024,384]{1,0:T(8,128)(2,1)S(1)}, u32[]{:S(2)}, u32[]{:S(2)}) collective-permute-start(bf16[1024,384]{1,0:T(8,128)(2,1)S(1)} %get-tuple-element.13.refs_0_), channel_id=1, source_target_pairs={{0,1},{1,0},{2,3},{3,2},{4,5},{5,4},{6,7},{7,6},{8,9},{9,8},{10,11... | collective-permute-start | bytes 2359304 | tf_op jit(solution)/shard_map/ppermute | solution.py:23
  6.4 1.2 collective-permute-start.12
  7.6 4.3 %collective-permute-start = (bf16[8,384]{1,0:T(8,128)(2,1)S(1)}, bf16[8,384]{1,0:T(8,128)(2,1)S(1)}, u32[]{:S(2)}, u32[]{:S(2)}) collective-permute-start(bf16[8,384]{1,0:T(8,128)(2,1)S(1)} %get-tuple-element.11), channel_id=1, source_target_pairs={{0,4},{4,8},{8,12},{12,16},{16,20},{20,24},{24,28},{1,5},{5,9},{9,... | collective-permute-start | bytes 18440 | tf_op jit(solution)/shard_map/ppermute | solution.py:33
  12.0 1.9 %collective-permute-start.1 = (bf16[8,384]{1,0:T(8,128)(2,1)S(1)}, bf16[8,384]{1,0:T(8,128)(2,1)S(1)}, u32[]{:S(2)}, u32[]{:S(2)}) collective-permute-start(bf16[8,384]{1,0:T(8,128)(2,1)S(1)} %get-tuple-element.12), channel_id=1, source_target_pairs={{4,0},{8,4},{12,8},{16,12},{20,16},{24,20},{28,24},{5,1},{9,5},{13... | collective-permute-start | bytes 18440 | tf_op jit(solution)/shard_map/ppermute | solution.py:33
  13.9 3.3 %collective-permute-done.1.head_ref = bf16[8,384]{1,0:T(8,128)(2,1)S(1)} collective-permute-done((bf16[8,384]{1,0:T(8,128)(2,1)S(1)}, bf16[8,384]{1,0:T(8,128)(2,1)S(1)}, u32[]{:S(2)}, u32[]{:S(2)}) %collective-permute-start.1) | collective-permute-done | bytes 6176 | tf_op jit(solution)/shard_map/ppermute | solution.py:33
  17.2 0.7 shard_map.96.refs_0_.refs_5_
  17.8 0.3 collective-permute-start.2
  18.2 0.2 collective-permute-start.3
  18.4 5.2 %collective-permute-done.11.refs_1_ = bf16[1024,384]{1,0:T(8,128)(2,1)S(1)} collective-permute-done((bf16[1024,384]{1,0:T(8,128)(2,1)S(1)}, bf16[1024,384]{1,0:T(8,128)(2,1)S(1)}, u32[]{:S(2)}, u32[]{:S(2)}) %collective-permute-start.11) | collective-permute-done | bytes 786464 | tf_op jit(solution)/shard_map/ppermute | solution.py:23
  23.6 0.8 slice.53
  24.5 1.2 collective-permute-start.13
  25.7 0.9 slice.54
  26.5 1.2 collective-permute-start.14
  27.8 13.0 %collective-permute-done.2.refs_1_.refs_6_ = bf16[1040,384]{1,0:T(8,128)(2,1)S(1)} collective-permute-done((bf16[1040,384]{1,0:T(8,128)(2,1)S(1)}, bf16[1040,384]{1,0:T(8,128)(2,1)S(1)}, u32[]{:S(2)}, u32[]{:S(2)}) %collective-permute-start.2) | collective-permute-done | bytes 798752 | tf_op jit(solution)/shard_map/ppermute | solution.py:23
  40.8 0.8 slice.48
  41.6 1.2 collective-permute-start.4
  42.8 0.0 collective-permute-done.3.refs_2_.refs_7_
  42.8 0.8 slice.49
  43.6 0.9 copy-done.6
  44.5 1.2 collective-permute-start.5
  45.7 0.2 collective-permute-start.6
  45.9 13.0 %collective-permute-done.6.refs_5_.refs_8_ = bf16[16,384]{1,0:T(8,128)(2,1)S(1)} collective-permute-done((bf16[16,384]{1,0:T(8,128)(2,1)S(1)}, bf16[16,384]{1,0:T(8,128)(2,1)S(1)}, u32[]{:S(2)}, u32[]{:S(2)}) %collective-permute-start.6) | collective-permute-done | bytes 12320 | tf_op jit(solution)/shard_map/ppermute | solution.py:23
  58.9 0.0 collective-permute-done.13.refs_3_
  58.9 1.1 copy-done.3
  60.0 1.1 copy-done.5
  61.2 1.1 copy-done.7
  62.3 2.0 %copy-done.12 = bf16[3,1536,384]{2,1,0:T(8,128)(2,1)S(1)} copy-done((bf16[3,1536,384]{2,1,0:T(8,128)(2,1)S(1)}, bf16[3,1536,384]{2,1,0:T(8,128)(2,1)}, u32[]{:S(2)}) %copy-start.12) | copy-done | bytes 3538968
  64.3 1.1 copy-done.15
  65.4 5.6 %shard_map.98.refs_0_ = bf16[1024,384]{1,0:T(8,128)(2,1)S(1)} custom-call(s32[1]{0:T(128)} %bitcast.t_ref, bf16[4,512,384]{2,1,0:T(8,128)(2,1)S(1)} %copy-done.1, bf16[3,1536,384]{2,1,0:T(8,128)(2,1)S(1)} %copy-done.12, bf16[1024,384]{1,0:T(8,128)(2,1)S(1)} %copy-done.15, bf16[1024,384]{1,0:T(8,128)(2,1)S(1)} %copy-done.3, bf16[1024,384]{1,0:T(8,128)(2,1)S(1)} %copy-done.5, ...), custom_call_target="tpu_custom_call" | custom-call | flops 3623878656 | bytes 6684672 | tf_op jit(solution)/shard_map/pallas_call | solution.py:238
  71.1 0.0 copy-start.11
  71.1 0.0 copy-start.17
  71.1 0.0 copy-start.13
  71.1 0.0 copy-start.16
  71.1 0.4 collective-permute-start.15
  71.5 1.1 collective-permute-start.16
  72.7 5.5 %shard_map.97.refs_0_ = bf16[1024,384]{1,0:T(8,128)(2,1)S(1)} custom-call(s32[1]{0:T(128)} %bitcast.t_ref, bf16[4,512,384]{2,1,0:T(8,128)(2,1)S(1)} %copy-done.1, bf16[3,1536,384]{2,1,0:T(8,128)(2,1)S(1)} %copy-done.12, bf16[1040,384]{1,0:T(8,128)(2,1)S(1)} %shard_map.96.refs_0_.refs_5_, bf16[1040,384]{1,0:T(8,128)(2,1)S(1)} %collective-permute-done.2.refs_1_.refs_6_, ...), custom_call_target="tpu_custom_call" | custom-call | flops 3623878656 | bytes 6684672 | tf_op jit(solution)/shard_map/pallas_call | solution.py:238
  78.2 0.7 collective-permute-start.8
  78.9 0.8 collective-permute-start.7
  79.7 8.9 %collective-permute-done.15.refs_1_ = bf16[1024,384]{1,0:T(8,128)(2,1)S(1)} collective-permute-done((bf16[1024,384]{1,0:T(8,128)(2,1)S(1)}, bf16[1024,384]{1,0:T(8,128)(2,1)S(1)}, u32[]{:S(2)}, u32[]{:S(2)}) %collective-permute-start.15) | collective-permute-done | bytes 786464 | tf_op jit(solution)/shard_map/ppermute | solution.py:23
  88.6 1.3 collective-permute-start.17
  90.0 0.3 collective-permute-start.18
  90.3 0.1 convert_reduce_fusion
  90.4 0.1 slice.47
  90.5 7.4 %collective-permute-start.20 = (f32[4]{0:T(128)S(1)}, f32[4]{0:T(128)S(1)}, u32[]{:S(2)}, u32[]{:S(2)}) collective-permute-start(f32[4]{0:T(128)S(1)} %slice.47), channel_id=1, source_target_pairs={{4,0},{8,4},{12,8},{16,12},{20,16},{24,20},{28,24},{5,1},{9,5},{13... | collective-permute-start | bytes 56 | tf_op jit(solution)/shard_map/ppermute | solution.py:33
  97.9 7.9 %collective-permute-done.8.refs_2_ = bf16[1024,384]{1,0:T(8,128)(2,1)S(1)} collective-permute-done((bf16[1024,384]{1,0:T(8,128)(2,1)S(1)}, bf16[1024,384]{1,0:T(8,128)(2,1)S(1)}, u32[]{:S(2)}, u32[]{:S(2)}) %collective-permute-start.8) | collective-permute-done | bytes 786464 | tf_op jit(solution)/shard_map/ppermute | solution.py:23
  105.8 0.9 collective-permute-start.10
  106.8 1.3 collective-permute-start.9
  108.1 0.0 collective-permute-done.20
  108.1 0.1 select_reduce_fusion
  108.2 6.0 %collective-permute-done.17.refs_3_ = bf16[512,384]{1,0:T(8,128)(2,1)S(1)} collective-permute-done((bf16[512,384]{1,0:T(8,128)(2,1)S(1)}, bf16[512,384]{1,0:T(8,128)(2,1)S(1)}, u32[]{:S(2)}, u32[]{:S(2)}) %collective-permute-start.17) | collective-permute-done | bytes 393248 | tf_op jit(solution)/shard_map/ppermute | solution.py:23
  114.2 5.7 %shard_map.99 = (bf16[4,512,1024]{2,1,0:T(8,128)(2,1)}, f32[32,1024]{1,0:T(8,128)S(1)}, f32[8,1024]{1,0:T(8,128)S(1)}) custom-call(s32[1]{0:T(128)} %bitcast.t_ref, bf16[1536,1024]{1,0:T(8,128)(2,1)S(1)} %copy-done.13, f32[1024]{0:T(1024)S(1)} %copy-done.16, s32[4,512]{1,0:T(4,128)S(1)} %copy-done.11, bf16[1024,384]{1,0:T(8,128)(2,1)S(1)} %shard_map.98.refs_0_, ...), custom_call_target="tpu_custom_call" | custom-call | flops 3221225472 | bytes 8388608 | tf_op jit(solution)/shard_map/pallas_call | solution.py:258
  120.0 2.3 %collective-permute-done.10.refs_4_ = bf16[512,384]{1,0:T(8,128)(2,1)S(1)} collective-permute-done((bf16[512,384]{1,0:T(8,128)(2,1)S(1)}, bf16[512,384]{1,0:T(8,128)(2,1)S(1)}, u32[]{:S(2)}, u32[]{:S(2)}) %collective-permute-start.10) | collective-permute-done | bytes 393248 | tf_op jit(solution)/shard_map/ppermute | solution.py:23
  122.3 0.4 collective-permute-done.9.refs_3_
  122.6 6.0 %shard_map.100 = (bf16[4,512,1024]{2,1,0:T(8,128)(2,1)}, f32[32,1024]{1,0:T(8,128)S(1)}, f32[8,1024]{1,0:T(8,128)S(1)}) custom-call(s32[1]{0:T(128)} %bitcast.t_ref, bf16[1536,1024]{1,0:T(8,128)(2,1)S(1)} %copy-done.13, f32[1024]{0:T(1024)S(1)} %copy-done.16, s32[4,512]{1,0:T(4,128)S(1)} %copy-done.11, ...), custom_call_target="tpu_custom_call", output_to_operand_aliasing={{0}: (11, {})} | custom-call | flops 3221225472 | bytes 8388608 | tf_op jit(solution)/shard_map/pallas_call | solution.py:258
  128.6 4.5 %collective-permute-start.19 = (f32[8,1024]{1,0:T(8,128)S(1)}, f32[8,1024]{1,0:T(8,128)S(1)}, u32[]{:S(2)}, u32[]{:S(2)}) collective-permute-start(f32[8,1024]{1,0:T(8,128)S(1)} %get-tuple-element.19), channel_id=1, source_target_pairs={{4,0},{8,4},{12,8},{16,12},{20,16},{24,20},{28,24},{5,1},{9,5},{13... | collective-permute-start | bytes 98312 | tf_op jit(solution)/shard_map/ppermute | solution.py:33
  133.1 2.6 %collective-permute-done.19 = f32[8,1024]{1,0:T(8,128)S(1)} collective-permute-done((f32[8,1024]{1,0:T(8,128)S(1)}, f32[8,1024]{1,0:T(8,128)S(1)}, u32[]{:S(2)}, u32[]{:S(2)}) %collective-permute-start.19) | collective-permute-done | bytes 32800 | tf_op jit(solution)/shard_map/ppermute | solution.py:33
  135.8 0.3 fusion
  136.1 0.7 add_divide_fusion
  (36 shorter events, 0.2 us)
Async XLA Ops:
  0.6 1.4 %copy-start = (bf16[4,512,384]{2,1,0:T(8,128)(2,1)S(1)}, bf16[4,512,384]{2,1,0:T(8,128)(2,1)}, u32[]{:S(2)}) copy-start(bf16[4,512,384]{2,1,0:T(8,128)(2,1)} %act_ref.7) | copy-start | bytes 4718596
  2.0 0.7 copy-start.9
  2.7 0.7 copy-start.10
  4.3 41.4 %copy-start.14 = (bf16[1024,384]{1,0:T(8,128)(2,1)}, bf16[1024,384]{1,0:T(8,128)(2,1)S(1)}, u32[]{:S(2)}) copy-start(bf16[1024,384]{1,0:T(8,128)(2,1)S(1)} %get-tuple-element.13.refs_0_) | copy-start | bytes 2359300
  4.3 54.6 %copy-start.1 = (bf16[4,512,384]{2,1,0:T(8,128)(2,1)S(1)}, bf16[4,512,384]{2,1,0:T(8,128)(2,1)}, u32[]{:S(2)}) copy-start(bf16[4,512,384]{2,1,0:T(8,128)(2,1)} %act_ref.7) | copy-start | bytes 4718596
  4.3 19.3 %collective-permute-start.11 = (bf16[1024,384]{1,0:T(8,128)(2,1)S(1)}, bf16[1024,384]{1,0:T(8,128)(2,1)S(1)}, u32[]{:S(2)}, u32[]{:S(2)}) collective-permute-start(bf16[1024,384]{1,0:T(8,128)(2,1)S(1)} %get-tuple-element.13.refs_0_), channel_id=1, source_target_pairs={{0,1},{1,0},{2,3},{3,2},{4,5},{5,4},{6,7},{7,6},{8,9},{9,8},{10,11... | collective-permute-start | bytes 2359304 | tf_op jit(solution)/shard_map/ppermute | solution.py:23
  6.4 19.3 %collective-permute-start.12 = (bf16[1024,384]{1,0:T(8,128)(2,1)S(1)}, bf16[1024,384]{1,0:T(8,128)(2,1)S(1)}, u32[]{:S(2)}, u32[]{:S(2)}) collective-permute-start(bf16[1024,384]{1,0:T(8,128)(2,1)S(1)} %get-tuple-element.13.refs_0_), channel_id=1, source_target_pairs={{0,2},{1,3},{2,0},{3,1},{4,6},{5,7},{6,4},{7,5},{8,10},{9,11},{10,... | collective-permute-start | bytes 2359304 | tf_op jit(solution)/shard_map/ppermute | solution.py:23
  7.6 6.3 %collective-permute-start = (bf16[8,384]{1,0:T(8,128)(2,1)S(1)}, bf16[8,384]{1,0:T(8,128)(2,1)S(1)}, u32[]{:S(2)}, u32[]{:S(2)}) collective-permute-start(bf16[8,384]{1,0:T(8,128)(2,1)S(1)} %get-tuple-element.11), channel_id=1, source_target_pairs={{0,4},{4,8},{8,12},{12,16},{16,20},{20,24},{24,28},{1,5},{5,9},{9,... | collective-permute-start | bytes 18440 | tf_op jit(solution)/shard_map/ppermute | solution.py:33
  12.0 5.2 %collective-permute-start.1 = (bf16[8,384]{1,0:T(8,128)(2,1)S(1)}, bf16[8,384]{1,0:T(8,128)(2,1)S(1)}, u32[]{:S(2)}, u32[]{:S(2)}) collective-permute-start(bf16[8,384]{1,0:T(8,128)(2,1)S(1)} %get-tuple-element.12), channel_id=1, source_target_pairs={{4,0},{8,4},{12,8},{16,12},{20,16},{24,20},{28,24},{5,1},{9,5},{13... | collective-permute-start | bytes 18440 | tf_op jit(solution)/shard_map/ppermute | solution.py:33
  17.8 22.9 %collective-permute-start.2 = (bf16[1040,384]{1,0:T(8,128)(2,1)S(1)}, bf16[1040,384]{1,0:T(8,128)(2,1)S(1)}, u32[]{:S(2)}, u32[]{:S(2)}) collective-permute-start(bf16[1040,384]{1,0:T(8,128)(2,1)S(1)} %shard_map.96.refs_0_.refs_5_), channel_id=1, source_target_pairs={{0,1},{1,0},{2,3},{3,2},{4,5},{5,4},{6,7},{7,6},{8,9},{9,8},{10,11... | collective-permute-start | bytes 2396168 | tf_op jit(solution)/shard_map/ppermute | solution.py:23
  18.2 24.6 %collective-permute-start.3 = (bf16[1040,384]{1,0:T(8,128)(2,1)S(1)}, bf16[1040,384]{1,0:T(8,128)(2,1)S(1)}, u32[]{:S(2)}, u32[]{:S(2)}) collective-permute-start(bf16[1040,384]{1,0:T(8,128)(2,1)S(1)} %shard_map.96.refs_0_.refs_5_), channel_id=1, source_target_pairs={{0,2},{1,3},{2,0},{3,1},{4,6},{5,7},{6,4},{7,5},{8,10},{9,11},{10,... | collective-permute-start | bytes 2396168 | tf_op jit(solution)/shard_map/ppermute | solution.py:23
  23.6 19.1 %copy-start.2 = (bf16[1024,384]{1,0:T(8,128)(2,1)}, bf16[1024,384]{1,0:T(8,128)(2,1)S(1)}, u32[]{:S(2)}) copy-start(bf16[1024,384]{1,0:T(8,128)(2,1)S(1)} %collective-permute-done.11.refs_1_) | copy-start | bytes 2359300
  24.5 34.4 %collective-permute-start.13 = (bf16[512,384]{1,0:T(8,128)(2,1)}, bf16[512,384]{1,0:T(8,128)(2,1)}, u32[]{:S(2)}, u32[]{:S(2)}) collective-permute-start(bf16[512,384]{1,0:T(8,128)(2,1)} %slice.53), channel_id=1, source_target_pairs={{0,2},{1,3},{2,0},{3,1},{4,6},{5,7},{6,4},{7,5},{8,10},{9,11},{10,... | collective-permute-start | bytes 1179656 | tf_op jit(solution)/shard_map/ppermute | solution.py:23
  25.7 17.9 %copy-start.4 = (bf16[1024,384]{1,0:T(8,128)(2,1)}, bf16[1024,384]{1,0:T(8,128)(2,1)S(1)}, u32[]{:S(2)}) copy-start(bf16[1024,384]{1,0:T(8,128)(2,1)S(1)} %collective-permute-done.12.refs_2_) | copy-start | bytes 2359300
  26.5 32.3 %collective-permute-start.14 = (bf16[512,384]{1,0:T(8,128)(2,1)}, bf16[512,384]{1,0:T(8,128)(2,1)}, u32[]{:S(2)}, u32[]{:S(2)}) collective-permute-start(bf16[512,384]{1,0:T(8,128)(2,1)} %slice.54), channel_id=1, source_target_pairs={{0,1},{1,0},{2,3},{3,2},{4,5},{5,4},{6,7},{7,6},{8,9},{9,8},{10,11... | collective-permute-start | bytes 1179656 | tf_op jit(solution)/shard_map/ppermute | solution.py:23
  41.6 31.1 %collective-permute-start.4 = (bf16[512,384]{1,0:T(8,128)(2,1)}, bf16[512,384]{1,0:T(8,128)(2,1)}, u32[]{:S(2)}, u32[]{:S(2)}) collective-permute-start(bf16[512,384]{1,0:T(8,128)(2,1)} %slice.48), channel_id=1, source_target_pairs={{0,2},{1,3},{2,0},{3,1},{4,6},{5,7},{6,4},{7,5},{8,10},{9,11},{10,... | collective-permute-start | bytes 1179656 | tf_op jit(solution)/shard_map/ppermute | solution.py:23
  43.6 0.9 copy-start.6
  44.5 28.2 %collective-permute-start.5 = (bf16[512,384]{1,0:T(8,128)(2,1)}, bf16[512,384]{1,0:T(8,128)(2,1)}, u32[]{:S(2)}, u32[]{:S(2)}) collective-permute-start(bf16[512,384]{1,0:T(8,128)(2,1)} %slice.49), channel_id=1, source_target_pairs={{0,1},{1,0},{2,3},{3,2},{4,5},{5,4},{6,7},{7,6},{8,9},{9,8},{10,11... | collective-permute-start | bytes 1179656 | tf_op jit(solution)/shard_map/ppermute | solution.py:23
  45.7 13.2 %collective-permute-start.6 = (bf16[16,384]{1,0:T(8,128)(2,1)S(1)}, bf16[16,384]{1,0:T(8,128)(2,1)S(1)}, u32[]{:S(2)}, u32[]{:S(2)}) collective-permute-start(bf16[16,384]{1,0:T(8,128)(2,1)S(1)} %slice.50), channel_id=1, source_target_pairs={{0,2},{1,3},{2,0},{3,1},{4,6},{5,7},{6,4},{7,5},{8,10},{9,11},{10,... | collective-permute-start | bytes 36872 | tf_op jit(solution)/shard_map/ppermute | solution.py:23
  58.9 1.1 copy-start.3
  60.0 1.1 copy-start.5
  61.2 1.1 copy-start.7
  62.3 2.0 %copy-start.12 = (bf16[3,1536,384]{2,1,0:T(8,128)(2,1)S(1)}, bf16[3,1536,384]{2,1,0:T(8,128)(2,1)}, u32[]{:S(2)}) copy-start(bf16[3,1536,384]{2,1,0:T(8,128)(2,1)} %w_ref.5) | copy-start | bytes 10616836
  64.3 1.1 copy-start.15
  65.4 7.2 %copy-start.8 = (bf16[1040,384]{1,0:T(8,128)(2,1)S(1)}, bf16[1040,384]{1,0:T(8,128)(2,1)}, u32[]{:S(2)}) copy-start(bf16[1040,384]{1,0:T(8,128)(2,1)} %copy-done.6) | copy-start | bytes 2396164
  71.1 19.2 %copy-start.11 = (s32[4,512]{1,0:T(4,128)S(1)}, s32[4,512]{1,0:T(4,128)}, u32[]{:S(2)}) copy-start(s32[4,512]{1,0:T(4,128)} %slot_ref.3) | copy-start | bytes 24580
  71.1 37.0 %copy-start.17 = (s32[4]{0:T(128)S(1)}, s32[4]{0:T(128)}, u32[]{:S(2)}) copy-start(s32[4]{0:T(128)} %param.15) | copy-start | bytes 52
  71.1 43.1 %copy-start.13 = (bf16[1536,1024]{1,0:T(8,128)(2,1)S(1)}, bf16[1536,1024]{1,0:T(8,128)(2,1)}, u32[]{:S(2)}) copy-start(bf16[1536,1024]{1,0:T(8,128)(2,1)} %w_ref.7) | copy-start | bytes 9437188
  71.1 43.1 %copy-start.16 = (f32[1024]{0:T(1024)S(1)}, f32[1024]{0:T(1024)}, u32[]{:S(2)}) copy-start(f32[1024]{0:T(1024)} %bias_ref.7) | copy-start | bytes 12292
  71.1 17.5 %collective-permute-start.15 = (bf16[1024,384]{1,0:T(8,128)(2,1)S(1)}, bf16[1024,384]{1,0:T(8,128)(2,1)S(1)}, u32[]{:S(2)}, u32[]{:S(2)}) collective-permute-start(bf16[1024,384]{1,0:T(8,128)(2,1)S(1)} %shard_map.98.refs_0_), channel_id=1, source_target_pairs={{0,1},{1,0},{2,3},{3,2},{4,5},{5,4},{6,7},{7,6},{8,9},{9,8},{10,11... | collective-permute-start | bytes 2359304 | tf_op jit(solution)/shard_map/ppermute | solution.py:23
  71.5 18.4 %collective-permute-start.16 = (bf16[1024,384]{1,0:T(8,128)(2,1)S(1)}, bf16[1024,384]{1,0:T(8,128)(2,1)S(1)}, u32[]{:S(2)}, u32[]{:S(2)}) collective-permute-start(bf16[1024,384]{1,0:T(8,128)(2,1)S(1)} %shard_map.98.refs_0_), channel_id=1, source_target_pairs={{0,2},{1,3},{2,0},{3,1},{4,6},{5,7},{6,4},{7,5},{8,10},{9,11},{10,... | collective-permute-start | bytes 2359304 | tf_op jit(solution)/shard_map/ppermute | solution.py:23
  78.2 27.6 %collective-permute-start.8 = (bf16[1024,384]{1,0:T(8,128)(2,1)S(1)}, bf16[1024,384]{1,0:T(8,128)(2,1)S(1)}, u32[]{:S(2)}, u32[]{:S(2)}) collective-permute-start(bf16[1024,384]{1,0:T(8,128)(2,1)S(1)} %shard_map.97.refs_0_), channel_id=1, source_target_pairs={{0,2},{1,3},{2,0},{3,1},{4,6},{5,7},{6,4},{7,5},{8,10},{9,11},{10,... | collective-permute-start | bytes 2359304 | tf_op jit(solution)/shard_map/ppermute | solution.py:23
  78.9 27.9 %collective-permute-start.7 = (bf16[1024,384]{1,0:T(8,128)(2,1)S(1)}, bf16[1024,384]{1,0:T(8,128)(2,1)S(1)}, u32[]{:S(2)}, u32[]{:S(2)}) collective-permute-start(bf16[1024,384]{1,0:T(8,128)(2,1)S(1)} %shard_map.97.refs_0_), channel_id=1, source_target_pairs={{0,1},{1,0},{2,3},{3,2},{4,5},{5,4},{6,7},{7,6},{8,9},{9,8},{10,11... | collective-permute-start | bytes 2359304 | tf_op jit(solution)/shard_map/ppermute | solution.py:23
  88.6 25.6 %collective-permute-start.17 = (bf16[512,384]{1,0:T(8,128)(2,1)S(1)}, bf16[512,384]{1,0:T(8,128)(2,1)S(1)}, u32[]{:S(2)}, u32[]{:S(2)}) collective-permute-start(bf16[512,384]{1,0:T(8,128)(2,1)S(1)} %slice.55), channel_id=1, source_target_pairs={{0,2},{1,3},{2,0},{3,1},{4,6},{5,7},{6,4},{7,5},{8,10},{9,11},{10,... | collective-permute-start | bytes 1179656 | tf_op jit(solution)/shard_map/ppermute | solution.py:23
  90.0 24.2 %collective-permute-start.18 = (bf16[512,384]{1,0:T(8,128)(2,1)S(1)}, bf16[512,384]{1,0:T(8,128)(2,1)S(1)}, u32[]{:S(2)}, u32[]{:S(2)}) collective-permute-start(bf16[512,384]{1,0:T(8,128)(2,1)S(1)} %slice.56), channel_id=1, source_target_pairs={{0,1},{1,0},{2,3},{3,2},{4,5},{5,4},{6,7},{7,6},{8,9},{9,8},{10,11... | collective-permute-start | bytes 1179656 | tf_op jit(solution)/shard_map/ppermute | solution.py:23
  90.5 17.6 %collective-permute-start.20 = (f32[4]{0:T(128)S(1)}, f32[4]{0:T(128)S(1)}, u32[]{:S(2)}, u32[]{:S(2)}) collective-permute-start(f32[4]{0:T(128)S(1)} %slice.47), channel_id=1, source_target_pairs={{4,0},{8,4},{12,8},{16,12},{20,16},{24,20},{28,24},{5,1},{9,5},{13... | collective-permute-start | bytes 56 | tf_op jit(solution)/shard_map/ppermute | solution.py:33
  105.8 16.4 %collective-permute-start.10 = (bf16[512,384]{1,0:T(8,128)(2,1)S(1)}, bf16[512,384]{1,0:T(8,128)(2,1)S(1)}, u32[]{:S(2)}, u32[]{:S(2)}) collective-permute-start(bf16[512,384]{1,0:T(8,128)(2,1)S(1)} %slice.52), channel_id=1, source_target_pairs={{0,1},{1,0},{2,3},{3,2},{4,5},{5,4},{6,7},{7,6},{8,9},{9,8},{10,11... | collective-permute-start | bytes 1179656 | tf_op jit(solution)/shard_map/ppermute | solution.py:23
  106.8 15.9 %collective-permute-start.9 = (bf16[512,384]{1,0:T(8,128)(2,1)S(1)}, bf16[512,384]{1,0:T(8,128)(2,1)S(1)}, u32[]{:S(2)}, u32[]{:S(2)}) collective-permute-start(bf16[512,384]{1,0:T(8,128)(2,1)S(1)} %slice.51), channel_id=1, source_target_pairs={{0,2},{1,3},{2,0},{3,1},{4,6},{5,7},{6,4},{7,5},{8,10},{9,11},{10,... | collective-permute-start | bytes 1179656 | tf_op jit(solution)/shard_map/ppermute | solution.py:23
  128.6 7.2 %collective-permute-start.19 = (f32[8,1024]{1,0:T(8,128)S(1)}, f32[8,1024]{1,0:T(8,128)S(1)}, u32[]{:S(2)}, u32[]{:S(2)}) collective-permute-start(f32[8,1024]{1,0:T(8,128)S(1)} %get-tuple-element.19), channel_id=1, source_target_pairs={{4,0},{8,4},{12,8},{16,12},{20,16},{24,20},{28,24},{5,1},{9,5},{13... | collective-permute-start | bytes 98312 | tf_op jit(solution)/shard_map/ppermute | solution.py:33

commit v2 on v0

v2 whole, which is shorter than its diff:
```python
import functools

import jax
import jax.numpy as jnp
from jax import lax
from jax.experimental import pallas as pl
from jax.experimental.pallas import tpu as pltpu
from jax.sharding import PartitionSpec as P


GENES_DEV = 32
LANES = 128
LIMIT = 16 << 20
EDGE = 16
SIDE = 8
VMEM = pl.BlockSpec(memory_space=pltpu.VMEM)
ANY = pl.BlockSpec(memory_space=pl.ANY)
HBM = pl.BlockSpec(memory_space=pltpu.HBM)
SMEM = pl.BlockSpec(memory_space=pltpu.SMEM)


def swap(value, bit):
    count = lax.axis_size("trk")
    return lax.ppermute(value, "trk", [(i, i ^ bit) for i in range(count)])


def swap_pos(value, bit):
    count = lax.axis_size("pos")
    return lax.ppermute(value, "pos", [(i, i ^ bit) for i in range(count)])


def split_bits(j):
    return j & -j, 1 << (j.bit_length() - 1)


def passed_along(value, axis, steps):
    count = lax.axis_size(axis)
    initial, last = (max(0, -steps), min(count, count - steps))
    return lax.ppermute(value, axis, [(source, source + steps) for source in range(initial, last)])


def gelu_of(values, gain, bias):
    return jax.nn.gelu(values.astype(jnp.float32) * gain + bias, approximate=True)


def params(**more):
    return pltpu.CompilerParams(vmem_limit_bytes=LIMIT, **more)


def cost(flops, nbytes, calls=0):
    return pl.CostEstimate(flops=int(flops), bytes_accessed=int(nbytes), transcendentals=int(calls))


def first_kernel(act_ref, gain_ref, bias_ref, *refs):
    sequences, length, channels = act_ref.shape
    outs = refs[:sequences]
    scale_ref, tail_ref, head_ref, edges, gain, bias, sems, edge_sems, scale_sems = refs[sequences:]
    copies = [
        pltpu.make_async_copy(act_ref.at[s], out.at[pl.ds(0, length)], sems.at[s]) for s, out in enumerate(outs)
    ]
    for s in range(sequences):
        for side, start in enumerate((length - EDGE, 0)):
            copies.append(
                pltpu.make_async_copy(act_ref.at[s, pl.ds(start, EDGE)], edges.at[s, side], edge_sems.at[s, side])
            )
    copies.append(pltpu.make_async_copy(gain_ref, gain, scale_sems.at[0]))
    copies.append(pltpu.make_async_copy(bias_ref, bias, scale_sems.at[1]))
    for copy in copies:
        copy.start()
    for copy in copies:
        copy.wait()
    index = lax.broadcasted_iota(jnp.int32, (SIDE, channels), 0)
    scale_ref[...] = jnp.where(index == 0, gain[...][None], bias[...][None])
    tails = jnp.zeros((SIDE, channels), jnp.float32)
    heads = tails
    for s in range(sequences):
        tails = jnp.where(index == s, edges[s, 0].astype(jnp.float32)[EDGE - 1 :], tails)
        heads = jnp.where(index == s, edges[s, 1].astype(jnp.float32)[:1], heads)
    tail_ref[...] = tails.astype(jnp.bfloat16)
    head_ref[...] = heads.astype(jnp.bfloat16)


def second_kernel(block_ref, before_ref, after_ref, out_ref, edges, sem):
    del block_ref
    edges[...] = jnp.concatenate(
        [before_ref[...].astype(jnp.float32), after_ref[...].astype(jnp.float32)]
    ).astype(jnp.bfloat16)
    copy = pltpu.make_async_copy(edges, out_ref.at[pl.ds(out_ref.shape[0] - EDGE, EDGE)], sem)
    copy.start()
    copy.wait()


def join_kernel(n_pieces, count, where_ref, *refs):
    pieces, out_ref, sems = refs[:n_pieces], refs[n_pieces], refs[n_pieces + 1]
    t, pos = where_ref[0], where_ref[1]
    taps, rows, channels = pieces[0].shape
    split = n_pieces // count
    copies = []
    for i, piece in enumerate(pieces):
        place = pos ^ i
        block = (place // split) ^ t
        start = pl.multiple_of((block * split + place % split) * rows, rows)
        for k in range(taps):
            copies.append(
                pltpu.make_async_copy(
                    piece.at[k],
                    out_ref.at[pl.ds(start, rows), pl.ds(k * channels, channels)],
                    sems.at[i, k],
                )
            )
            copies[-1].start()
    for copy in copies:
        copy.wait()


def stage_kernel(count, t_ref, w_ref, head_ref, w_out, head_out, sems):
    taps, _, channels = w_ref.shape
    copies = []
    for j in range(count):
        start = pl.multiple_of((t_ref[0] ^ j) * channels, channels)
        rows = pl.ds(j * channels, channels)
        for k in range(taps):
            copies.append(
                pltpu.make_async_copy(
                    w_ref.at[k, pl.ds(start, channels)],
                    w_out.at[rows, pl.ds(k * channels, channels)],
                    sems.at[j, k],
                )
            )
        copies.append(
            pltpu.make_async_copy(head_ref.at[pl.ds(start, channels)], head_out.at[rows], sems.at[j, taps])
        )
    for copy in copies:
        copy.start()
    for copy in copies:
        copy.wait()


def piece_kernel(pos_ref, w_ref, out_ref, sem):
    rows = out_ref.shape[1]
    start = pl.multiple_of(pos_ref[0] * rows, rows)
    copy = pltpu.make_async_copy(w_ref.at[:, pl.ds(start, rows)], out_ref, sem)
    copy.start()
    copy.wait()


def count_kernel(slot_ref, out_ref):
    sequences, length = slot_ref.shape
    index = lax.broadcasted_iota(jnp.int32, (out_ref.shape[0], length), 0)
    total = jnp.zeros((out_ref.shape[0], 1), jnp.float32)
    for s in range(sequences):
        hit = (index == slot_ref[s : s + 1, :]).astype(jnp.float32)
        total = total + jnp.sum(hit, axis=1, keepdims=True)
    out_ref[...] = jnp.broadcast_to(total, out_ref.shape)


def mean_kernel(map_ref, own_ref, got_ref, count_ref, got_count_ref, out_ref):
    n_own, width = own_ref.shape
    totals, counts = own_ref[...], count_ref[:n_own, :1]
    row = lax.broadcasted_iota(jnp.int32, (n_own, width), 0)
    short = row[:, :1]
    for s in range(map_ref.shape[0]):
        gene = map_ref[s]
        totals = totals + jnp.where(row == gene, got_ref[s : s + 1, :], 0.0)
        counts = counts + jnp.where(short == gene, got_count_ref[s : s + 1, :1], 0.0)
    out_ref[...] = totals / jnp.maximum(counts, 1.0)


def convolved(first, s, values, edge, weight, own):
    length, channels = own.shape
    made = jnp.dot(jnp.concatenate([values, edge]), weight, preferred_element_type=jnp.float32)
    row = lax.broadcasted_iota(jnp.int32, (length, channels), 0)
    before, at, after = (made[:, k * channels : (k + 1) * channels] for k in range(3))
    place = length + first + s
    left = jnp.where(row == 0, before[place : place + 1], pltpu.roll(before[:length], 1, 0))
    place += SIDE
    right = jnp.where(row == length - 1, after[place : place + 1], pltpu.roll(after[:length], length - 1, 0))
    return (own.astype(jnp.float32) + ((left + at[:length]) + right)).astype(jnp.bfloat16)


def conv_kernel(first, group, count, edge_at, ends_ref, w_ref, *refs):
    scales = refs[:count]
    blocks = [refs[count * (1 + s) : count * (2 + s)] for s in range(group)]
    refs = refs[count * (1 + group) :]
    if edge_at is None:
        edge_in, refs = refs[0], refs[1:]
    hidden_ref, refs = refs[0], refs[1:]
    if edge_at is not None:
        edge_out, refs = refs[0], refs[1:]
    outs = refs
    length = hidden_ref.shape[0] // group
    channels = scales[0].shape[1]
    weight = w_ref[...]
    gains = [(scale[0:1, :], scale[1:2, :]) for scale in scales]
    if edge_at is None:
        edge = edge_in[...]
    else:
        row = lax.broadcasted_iota(jnp.int32, (EDGE, channels), 0)
        alive = jnp.where(row < SIDE, ends_ref[0], ends_ref[1]) > 0
        edge = jnp.concatenate(
            [
                jnp.where(alive, gelu_of(blocks[edge_at][j][length : length + EDGE, :], *gains[j]), 0.0)
                for j in range(count)
            ],
            axis=1,
        ).astype(jnp.bfloat16)
        edge_out[...] = edge
    for s in range(group):
        values = jnp.concatenate(
            [gelu_of(blocks[s][j][:length, :], *gains[j]).astype(jnp.bfloat16) for j in range(count)], axis=1
        )
        hidden_ref[s * length : (s + 1) * length, :] = values
        made = convolved(first, s, values, edge, weight, blocks[s][0][:length, :])
        if len(outs) == 1:
            outs[0][s * length : (s + 1) * length, :] = made
        else:
            outs[s][...] = made


def again_kernel(first, group, w_ref, edge_ref, hidden_ref, *refs):
    own, out_ref = refs[:group], refs[group]
    length = hidden_ref.shape[0] // group
    weight = w_ref[...]
    for s in range(group):
        rows = slice(s * length, (s + 1) * length)
        out_ref[rows, :] = convolved(
            first, s, hidden_ref[rows, :], edge_ref[...], weight, own[s][:length, :]
        )


def head_kernel(first, plan, n_blocks, more, w_ref, bias_ref, slot_ref, *refs):
    blocks = refs[:n_blocks]
    refs = refs[n_blocks:]
    if more:
        own_in, strad_in, _ = refs[:3]
        refs = refs[3:]
    tracks_ref, own_ref, strad_ref, made, out_sems = refs
    length = made.shape[1]
    weight = w_ref[...]
    n_own, n_strad = own_ref.shape[0], strad_ref.shape[0]
    index = lax.broadcasted_iota(jnp.int32, (n_own + n_strad, length), 0)
    if more:
        sums = jnp.concatenate([own_in[...], strad_in[...]])
    else:
        sums = jnp.zeros((n_own + n_strad, w_ref.shape[1]), jnp.float32)
    bias = bias_ref[...][None]
    outs = []
    for s, places in enumerate(plan):
        values = jnp.concatenate([blocks[which][row : row + length, :] for which, row in places], axis=1)
        logits = jnp.dot(values, weight, preferred_element_type=jnp.float32) + bias
        part = jnp.maximum(logits, 0.0) + jnp.log1p(jnp.exp(-jnp.abs(logits)))
        made[s] = part.astype(jnp.bfloat16)
        outs.append(pltpu.make_async_copy(made.at[s], tracks_ref.at[first + s], out_sems.at[s]))
        outs[-1].start()
        onehot = (index == slot_ref[first + s : first + s + 1, :]).astype(jnp.bfloat16)
        sums = sums + jnp.dot(onehot, made[s], preferred_element_type=jnp.float32)
    own_ref[...] = sums[:n_own]
    strad_ref[...] = sums[n_own:]
    for copy in outs:
        copy.wait()


def by_kernels(
    activations, norm_gain, norm_bias, conv_weight, head_weight, head_bias, gene_slot, straddle_map
):
    sequences, length, channels = activations.shape
    count, n_pos = lax.axis_size("trk"), lax.axis_size("pos")
    pos = lax.axis_index("pos").astype(jnp.int32)
    t = lax.axis_index("trk").astype(jnp.int32)
    where = jnp.stack([t, pos])
    ends = jnp.stack([(pos > 0).astype(jnp.int32), (pos < n_pos - 1).astype(jnp.int32)])
    whole = channels * count
    n_tracks = head_weight.shape[1]
    group = sequences // 2
    rows = group * length
    bf16, f32 = jnp.bfloat16, jnp.float32
    Shape = jax.ShapeDtypeStruct
    far = [j for j in range(count) if j & (j - 1)]

    piece = whole // n_pos
    mine = pl.pallas_call(
        piece_kernel,
        out_shape=Shape((3, piece, channels), bf16),
        in_specs=[SMEM, ANY],
        out_specs=VMEM,
        scratch_shapes=[pltpu.SemaphoreType.DMA],
        cost_estimate=cost(0, 12 * piece * channels),
    )(pos[None], conv_weight)
    far_weights = {}
    for j in far:
        pieces = {0: swap(mine, j)}
        bit = 2
        while bit < 2 * n_pos:
            step = bit if bit < n_pos else 1
            for i in sorted(pieces):
                pieces[i ^ step] = swap_pos(pieces[i], step)
            bit *= 2
        far_weights[j] = pl.pallas_call(
            functools.partial(join_kernel, n_pos, count),
            out_shape=Shape((whole, 3 * channels), bf16),
            in_specs=[SMEM] + [ANY] * n_pos,
            out_specs=VMEM,
            scratch_shapes=[pltpu.SemaphoreType.DMA((n_pos, 3))],
            compiler_params=params(),
            cost_estimate=cost(0, 12 * whole * channels),
        )(where, *(pieces[i] for i in range(n_pos)))

    taps, heads = pl.pallas_call(
        functools.partial(stage_kernel, count),
        out_shape=[Shape((whole, 3 * channels), bf16), Shape((whole, n_tracks), bf16)],
        in_specs=[SMEM, ANY, ANY],
        out_specs=[VMEM, VMEM],
        scratch_shapes=[pltpu.SemaphoreType.DMA((count, 4))],
        compiler_params=params(),
        cost_estimate=cost(0, 4 * whole * (3 * channels + n_tracks)),
    )(where, conv_weight, head_weight)

    edged = 1
    *blocks, scale, tails, fronts = pl.pallas_call(
        first_kernel,
        out_shape=[Shape((length + EDGE * (s == edged), channels), bf16) for s in range(sequences)]
        + [Shape((SIDE, channels), f32), Shape((SIDE, channels), bf16), Shape((SIDE, channels), bf16)],
        in_specs=[ANY] * 3,
        out_specs=[VMEM] * (sequences + 3),
        scratch_shapes=[
            pltpu.VMEM((sequences, 2, EDGE, channels), bf16),
            pltpu.VMEM((channels,), f32),
            pltpu.VMEM((channels,), f32),
            pltpu.SemaphoreType.DMA((sequences,)),
            pltpu.SemaphoreType.DMA((sequences, 2)),
            pltpu.SemaphoreType.DMA((2,)),
        ],
        cost_estimate=cost(0, 4 * sequences * length * channels),
    )(activations, norm_gain, norm_bias)
    before, after = passed_along(tails, "pos", 1), passed_along(fronts, "pos", -1)
    scales = [scale] + [swap(scale, j) for j in range(1, count)]
    blocks[edged] = pl.pallas_call(
        second_kernel,
        out_shape=Shape((length + EDGE, channels), bf16),
        in_specs=[ANY, VMEM, VMEM],
        out_specs=ANY,
        input_output_aliases={0: 0},
        scratch_shapes=[pltpu.VMEM((EDGE, channels), bf16), pltpu.SemaphoreType.DMA],
        compiler_params=params(),
        cost_estimate=cost(0, 4 * EDGE * channels),
    )(blocks[edged], before, after)
    near = []
    for s in range(sequences):
        found = {0: blocks[s]}
        for j in range(1, count):
            if j not in far:
                found[j] = swap(blocks[s], j)
        for j in far:
            step = split_bits(j)[1 - s % 2]
            found[j] = swap(found[j ^ step], step)
        near.append([found[j] for j in range(count)])

    owned, others = [], []
    edge = None
    for i in range(2):
        seqs = range(i * group, (i + 1) * group)
        edge_at = edged if i == 0 else None
        n_out = 1 if i == 0 else group
        hidden, *made = pl.pallas_call(
            functools.partial(conv_kernel, i * group, group, count, edge_at),
            out_shape=[Shape((rows, whole), bf16)]
            + ([Shape((EDGE, whole), bf16)] if i == 0 else [])
            + [Shape((rows // n_out, channels), bf16)] * n_out,
            in_specs=[SMEM] + [VMEM] * (1 + count * (1 + group) + (i > 0)),
            out_specs=[VMEM] * (1 + (i == 0) + n_out),
            compiler_params=params(),
            cost_estimate=cost(
                6 * rows * whole * channels, 2 * rows * whole + 6 * whole * channels, rows * whole
            ),
        )(ends, taps, *scales, *(block for s in seqs for block in near[s]), *([edge] if i else []))
        if i == 0:
            edge, *made = made
        owned.append(made)
        others.append(
            {
                j: pl.pallas_call(
                    functools.partial(again_kernel, i * group, group),
                    out_shape=Shape((rows, channels), bf16),
                    in_specs=[VMEM] * (3 + group),
                    out_specs=VMEM,
                    compiler_params=params(),
                    cost_estimate=cost(6 * rows * whole * channels, 2 * rows * whole + 6 * whole * channels),
                )(far_weights[j], edge, hidden, *(near[s][j] for s in seqs))
                for j in far
            }
        )

    stride = straddle_map.shape[0]
    n_strad = -(-stride // 8) * 8
    counts = pl.pallas_call(
        count_kernel,
        out_shape=Shape((GENES_DEV + n_strad, LANES), f32),
        in_specs=[VMEM],
        out_specs=VMEM,
        compiler_params=params(),
        cost_estimate=cost(sequences * length * GENES_DEV, 4 * sequences * length),
    )(gene_slot)
    got_counts = passed_along(counts[GENES_DEV:], "pos", -1)
    tracks, sums, done = None, (), 0
    for i in range(2):
        for part, own in enumerate(owned[i]):
            n_seqs = own.shape[0] // length
            arrays = [own] + [others[i][j] if j in far else swap(own, j) for j in range(1, count)]
            plan = [
                [(j, s * length + (part * n_seqs * length if j in far else 0)) for j in range(count)]
                for s in range(n_seqs)
            ]
            tracks, *sums = pl.pallas_call(
                functools.partial(head_kernel, done, plan, count, done > 0),
                out_shape=(
                    Shape((sequences, length, n_tracks), bf16),
                    Shape((GENES_DEV, n_tracks), f32),
                    Shape((n_strad, n_tracks), f32),
                ),
                in_specs=[VMEM] * (3 + count) + ([VMEM, VMEM, ANY] if done else []),
                out_specs=(ANY, VMEM, VMEM),
                input_output_aliases={5 + count: 0} if done else {},
                scratch_shapes=[
                    pltpu.VMEM((n_seqs, length, n_tracks), bf16),
                    pltpu.SemaphoreType.DMA((n_seqs,)),
                ],
                compiler_params=params(),
                cost_estimate=cost(
                    2 * n_seqs * length * whole * n_tracks,
                    2 * n_seqs * length * (whole + n_tracks) + 2 * whole * n_tracks,
                    2 * n_seqs * length * n_tracks,
                ),
            )(heads, head_bias, gene_slot, *arrays, *((*sums, tracks) if done else ()))
            done += n_seqs
    own, strad = sums
    gene_mean = pl.pallas_call(
        mean_kernel,
        out_shape=Shape((GENES_DEV, n_tracks), f32),
        in_specs=[SMEM] + [VMEM] * 4,
        out_specs=VMEM,
        compiler_params=params(),
        cost_estimate=cost(GENES_DEV * n_tracks, 12 * GENES_DEV * n_tracks),
    )(straddle_map, own, passed_along(strad, "pos", -1), counts, got_counts)
    return tracks, gene_mean


def by_ops(
    activations, norm_gain, norm_bias, conv_weight, head_weight, head_bias, gene_slot, straddle_map
):
    sequences, length, channels = activations.shape
    rows = sequences * length
    f32, bf16 = jnp.float32, jnp.bfloat16
    hidden = gelu_of(activations, norm_gain, norm_bias).astype(bf16)
    gathered = lax.all_gather(hidden, "trk", axis=2, tiled=True)
    padded = jnp.concatenate(
        [passed_along(gathered[:, -1:], "pos", 1), gathered, passed_along(gathered[:, :1], "pos", -1)], axis=1
    )
    total = jnp.zeros((rows, conv_weight.shape[2]), f32)
    for k in range(3):
        window = padded[:, k : k + length].reshape(rows, -1)
        total = total + jnp.dot(window, conv_weight[k], preferred_element_type=f32)
    mixed = (activations.reshape(rows, channels).astype(f32) + total).astype(bf16)
    mixed = lax.all_gather(mixed, "trk", axis=1, tiled=True)
    logits = jnp.dot(mixed, head_weight, preferred_element_type=f32)
    tracks = jax.nn.softplus(logits + head_bias).astype(bf16)
    slots = jnp.arange(GENES_DEV + straddle_map.shape[0], dtype=jnp.int32)
    onehot = (gene_slot.reshape(-1)[None, :] == slots[:, None]).astype(bf16)
    sums = jnp.dot(onehot, tracks, preferred_element_type=f32)
    mean = gene_mean_of(sums[:GENES_DEV], sums[GENES_DEV:], gene_slot, straddle_map)
    return tracks.reshape(sequences, length, -1), mean


def gene_mean_of(own, strad, gene_slot, straddle_map):
    stride = straddle_map.shape[0]
    f32 = jnp.float32
    slots = jnp.arange(GENES_DEV + stride, dtype=jnp.int32)
    counts = jnp.sum((gene_slot.reshape(-1)[None, :] == slots[:, None]).astype(f32), axis=1)
    received_counts = passed_along(counts[GENES_DEV:], "pos", -1)
    owners = (straddle_map[None, :] == jnp.arange(GENES_DEV, dtype=jnp.int32)[:, None]).astype(f32)
    gene_counts = counts[:GENES_DEV] + jnp.sum(owners * received_counts[None], axis=1)
    received = passed_along(strad, "pos", -1)[:stride]
    totals = own + jnp.dot(owners, received, precision=lax.Precision.HIGHEST)
    return totals / jnp.maximum(gene_counts, 1.0)[:, None]


def per_device(*args):
    piece = args[3].shape[1] // lax.axis_size("pos")
    lanes = args[0].shape[2] % LANES == 0 and args[4].shape[1] % LANES == 0 and piece % EDGE == 0
    return (by_kernels if lanes else by_ops)(*args)


def solution(mesh):
    in_specs = (
        P(None, "pos", "trk"),
        P("trk"),
        P("trk"),
        P(None, None, "trk"),
        P(None, "trk"),
        P("trk"),
        P(None, "pos"),
        P("pos"),
    )
    out_specs = (P(None, "pos", "trk"), P("pos", "trk"))
    return jax.shard_map(
        per_device, mesh=mesh, in_specs=in_specs, out_specs=out_specs, check_vma=False
    )
```

time: 204 us -> 152 us (0.75)
  waiting for transfers between devices: 142 us -> 50.5 us
  Pallas kernels: 0 us -> 47.7 us
  starting transfers between devices: 10.7 us -> 43.9 us
  matrix products: 28.1 us -> 0 us
  between operations: 14.3 us -> 1.04 us
  local copies, waits for them, and re-layouts: 1.12 us -> 8.58 us
  other arithmetic: 7.56 us -> 0.15 us
    all_gather x2 -> x0, waiting for transfers between devices: 139 us -> none  [the longest x1 71.9 us: per_device(): gathered = lax.all_gather(hidden, 'trk', axis=2, tiled=True)]
    pallas_call x0 -> x14, Pallas kernels: none -> 47.7 us  [the longest x2 13.9 us: by_kernels(): pl.pallas_call(functools.partial(conv_kernel, i * group, group, count, ed...]
    ppermute x2 -> x29, waiting for transfers between devices: 0.01 us -> 45.2 us  [the longest x22 36.3 us: swap(): return lax.ppermute(value, 'trk', [(i, i ^ bit) for i in range(count)])]
    dot_general x7 -> x0, matrix products: 28.1 us -> none  [the longest x3 13.9 us: per_device(): jnp.dot(window, tap_rows, preferred_element_type=jnp.float32)]
    ppermute x2 -> x29, starting transfers between devices: 5.76 us -> 32.2 us  [the longest x22 20.4 us: swap(): return lax.ppermute(value, 'trk', [(i, i ^ bit) for i in range(count)])]
    unnamed x19 -> x56, local copies, waits for them, and re-layouts: 0.06 us -> 8.58 us
    ppermute x2 -> x4, starting transfers between devices: 4.84 us -> 11.7 us  [passed_along(): lax.ppermute(value, axis, [(source, source + steps) for source in range(i...]
    convert_element_type x1 -> x0, other arithmetic: 4.03 us -> none  [per_device(): hidden = jax.nn.gelu(activations.astype(jnp.float32) * norm_gain + norm_b...]
  transfers between devices with their start and end apart: 6 -> 33, of which waited for: 3 -> 14; matrix products, arithmetic and copies ran while one was open for 10% -> 0% of each run, Pallas kernels for 0% -> 27%
where the time goes in v2:
time: 152 us
  waiting for transfers between devices  50.5 us (33%)
  Pallas kernels  47.7 us (31%)
  starting transfers between devices  43.9 us (29%)
  local copies, waits for them, and re-layouts  8.58 us (6%)
    ppermute x22, waiting for transfers between devices, swap(): return lax.ppermute(value, 'trk', [(i, i ^ bit) for i in range(count)])  36.3 us
    ppermute x22, starting transfers between devices, swap(): return lax.ppermute(value, 'trk', [(i, i ^ bit) for i in range(count)])  20.4 us
    pallas_call x2, Pallas kernels, by_kernels(): pl.pallas_call(functools.partial(conv_kernel, i * group, group, count, ed...  13.9 us
    pallas_call x3, Pallas kernels, by_kernels(): pl.pallas_call(functools.partial(head_kernel, done, plan, count, done > 0...  13.1 us
    ppermute x7, starting transfers between devices, swap_pos(): return lax.ppermute(value, 'pos', [(i, i ^ bit) for i in range(count)])  11.8 us
    ppermute x4, starting transfers between devices, passed_along(): lax.ppermute(value, axis, [(source, source + steps) for source in range(i...  11.7 us
    pallas_call x2, Pallas kernels, by_kernels(): pl.pallas_call(functools.partial(again_kernel, i * group, group), out_sha...  10.9 us
    ppermute x7, waiting for transfers between devices, swap_pos(): return lax.ppermute(value, 'pos', [(i, i ^ bit) for i in range(count)])  8.82 us
  transfers between devices with their start and end apart: 33, of which 14 were waited for; matrix products, arithmetic and copies ran while one was open for 0% of the time, Pallas kernels for 27%

profile of v2, /device:TPU:1, one launch (start us, length us, event | category | flops | bytes accessed | tf_op | source)
XLA Modules:
  0.0 151.9 jit_solution(13960592720215205140)
XLA Ops:
  0.6 1.9 %shard_map.100 = bf16[3,192,384]{2,1,0:T(8,128)(2,1)} custom-call(s32[1]{0:T(128)} %bitcast.1.pos_ref, bf16[3,1536,384]{2,1,0:T(8,128)(2,1)} %w_ref.3), custom_call_target="tpu_custom_call" | custom-call | bytes 884736 | tf_op jit(solution)/shard_map/pallas_call | solution.py:281
  2.6 3.0 %collective-permute-start.19 = (bf16[3,192,384]{2,1,0:T(8,128)(2,1)}, bf16[3,192,384]{2,1,0:T(8,128)(2,1)}, u32[]{:S(2)}, u32[]{:S(2)}) collective-permute-start(bf16[3,192,384]{2,1,0:T(8,128)(2,1)} %shard_map.100), channel_id=1, source_target_pairs={{0,3},{1,2},{2,1},{3,0},{4,7},{5,6},{6,5},{7,4},{8,11},{9,10},{10,... | collective-permute-start | bytes 1327112 | tf_op jit(solution)/shard_map/ppermute | solution.py:24
  5.6 2.8 %shard_map.96 = (bf16[512,384]{1,0:T(8,128)(2,1)}, bf16[528,384]{1,0:T(8,128)(2,1)}, bf16[512,384]{1,0:T(8,128)(2,1)}, bf16[512,384]{1,0:T(8,128)(2,1)}, f32[8,3...) custom-call(bf16[4,512,384]{2,1,0:T(8,128)(2,1)} %act_ref.1, f32[384]{0:T(512)} %gain_ref.1, f32[384]{0:T(512)} %bias_ref.4), custom_call_target="tpu_custom_call" | custom-call | bytes 3145728 | tf_op jit(solution)/shard_map/pallas_call | solution.py:319
  8.4 0.3 collective-permute-start.3
  8.8 4.8 %collective-permute-start.12 = (bf16[8,384]{1,0:T(8,128)(2,1)}, bf16[8,384]{1,0:T(8,128)(2,1)S(1)}, u32[]{:S(2)}, u32[]{:S(2)}) collective-permute-start(bf16[8,384]{1,0:T(8,128)(2,1)} %get-tuple-element.33), channel_id=1, source_target_pairs={{0,4},{4,8},{8,12},{12,16},{16,20},{20,24},{24,28},{1,5},{5,9},{9,... | collective-permute-start | bytes 18440 | tf_op jit(solution)/shard_map/ppermute | solution.py:39
  13.5 1.9 %collective-permute-start.13 = (bf16[8,384]{1,0:T(8,128)(2,1)}, bf16[8,384]{1,0:T(8,128)(2,1)S(1)}, u32[]{:S(2)}, u32[]{:S(2)}) collective-permute-start(bf16[8,384]{1,0:T(8,128)(2,1)} %get-tuple-element.34), channel_id=1, source_target_pairs={{4,0},{8,4},{12,8},{16,12},{20,16},{24,20},{28,24},{5,1},{9,5},{13... | collective-permute-start | bytes 18440 | tf_op jit(solution)/shard_map/ppermute | solution.py:39
  15.5 1.3 collective-permute-start
  16.8 2.3 %collective-permute-done.13.after_ref = bf16[8,384]{1,0:T(8,128)(2,1)S(1)} collective-permute-done((bf16[8,384]{1,0:T(8,128)(2,1)}, bf16[8,384]{1,0:T(8,128)(2,1)S(1)}, u32[]{:S(2)}, u32[]{:S(2)}) %collective-permute-start.13) | collective-permute-done | bytes 6176 | tf_op jit(solution)/shard_map/ppermute | solution.py:39
  19.1 1.2 collective-permute-start.6
  20.3 4.2 %collective-permute-done.refs_1_ = f32[8,384]{1,0:T(8,128)S(1)} collective-permute-done((f32[8,384]{1,0:T(8,128)}, f32[8,384]{1,0:T(8,128)S(1)}, u32[]{:S(2)}, u32[]{:S(2)}) %collective-permute-start) | collective-permute-done | bytes 12320 | tf_op jit(solution)/shard_map/ppermute | solution.py:24
  24.5 0.6 copy-done.22
  25.1 0.3 collective-permute-start.1
  25.5 2.7 %collective-permute-done.1.refs_2_ = f32[8,384]{1,0:T(8,128)S(1)} collective-permute-done((f32[8,384]{1,0:T(8,128)}, f32[8,384]{1,0:T(8,128)S(1)}, u32[]{:S(2)}, u32[]{:S(2)}) %collective-permute-start.1) | collective-permute-done | bytes 12320 | tf_op jit(solution)/shard_map/ppermute | solution.py:24
  28.2 0.6 copy-done.24
  28.8 1.2 collective-permute-start.2
  29.9 2.9 %collective-permute-done.2.refs_3_ = f32[8,384]{1,0:T(8,128)S(1)} collective-permute-done((f32[8,384]{1,0:T(8,128)}, f32[8,384]{1,0:T(8,128)S(1)}, u32[]{:S(2)}, u32[]{:S(2)}) %collective-permute-start.2) | collective-permute-done | bytes 12320 | tf_op jit(solution)/shard_map/ppermute | solution.py:24
  32.9 0.6 copy-done.26
  33.4 1.1 collective-permute-start.7
  34.6 1.2 collective-permute-start.9
  35.8 0.8 copy-done.12
  36.6 0.2 collective-permute-start.10
  36.8 1.3 collective-permute-start.21
  38.1 1.0 copy-done.2
  39.2 0.7 copy-done.15
  39.9 0.3 collective-permute-start.14
  40.2 0.4 collective-permute-done.7.refs_10_
  40.6 2.1 %collective-permute-start.15 = (bf16[528,384]{1,0:T(8,128)(2,1)S(1)}, bf16[528,384]{1,0:T(8,128)(2,1)}, u32[]{:S(2)}, u32[]{:S(2)}) collective-permute-start(bf16[528,384]{1,0:T(8,128)(2,1)S(1)} %shard_map.97.refs_8_), channel_id=1, source_target_pairs={{0,2},{1,3},{2,0},{3,1},{4,6},{5,7},{6,4},{7,5},{8,10},{9,11},{10,... | collective-permute-start | bytes 1216520 | tf_op jit(solution)/shard_map/ppermute | solution.py:24
  42.7 0.7 copy-done.3
  43.4 5.5 %collective-permute-done.10.refs_6_ = bf16[512,384]{1,0:T(8,128)(2,1)S(1)} collective-permute-done((bf16[512,384]{1,0:T(8,128)(2,1)}, bf16[512,384]{1,0:T(8,128)(2,1)S(1)}, u32[]{:S(2)}, u32[]{:S(2)}) %collective-permute-start.10) | collective-permute-done | bytes 393248 | tf_op jit(solution)/shard_map/ppermute | solution.py:24
  49.0 0.8 copy-done.19
  49.8 2.1 %collective-permute-start.11 = (bf16[512,384]{1,0:T(8,128)(2,1)}, bf16[512,384]{1,0:T(8,128)(2,1)}, u32[]{:S(2)}, u32[]{:S(2)}) collective-permute-start(bf16[512,384]{1,0:T(8,128)(2,1)} %collective-permute-done.9.refs_5_), channel_id=1, source_target_pairs={{0,2},{1,3},{2,0},{3,1},{4,6},{5,7},{6,4},{7,5},{8,10},{9,11},{10,... | collective-permute-start | bytes 1179656 | tf_op jit(solution)/shard_map/ppermute | solution.py:24
  51.9 0.8 copy-done.8
  52.6 1.9 %collective-permute-start.23 = (bf16[3,192,384]{2,1,0:T(8,128)(2,1)}, bf16[3,192,384]{2,1,0:T(8,128)(2,1)}, u32[]{:S(2)}, u32[]{:S(2)}) collective-permute-start(bf16[3,192,384]{2,1,0:T(8,128)(2,1)} %collective-permute-done.19.refs_0_), channel_id=1, source_target_pairs={{0,16},{4,20},{8,24},{12,28},{16,0},{20,4},{24,8},{28,12},{1,17},{... | collective-permute-start | bytes 1327112 | tf_op jit(solution)/shard_map/ppermute | solution.py:29
  54.5 0.5 collective-permute-start.25
  55.0 2.6 %collective-permute-done.15.refs_10_ = bf16[528,384]{1,0:T(8,128)(2,1)} collective-permute-done((bf16[528,384]{1,0:T(8,128)(2,1)S(1)}, bf16[528,384]{1,0:T(8,128)(2,1)}, u32[]{:S(2)}, u32[]{:S(2)}) %collective-permute-start.15) | collective-permute-done | bytes 405536 | tf_op jit(solution)/shard_map/ppermute | solution.py:24
  57.6 0.9 collective-permute-start.16
  58.6 7.5 %collective-permute-done.5.refs_7_.refs_0_ = bf16[512,384]{1,0:T(8,128)(2,1)} collective-permute-done((bf16[512,384]{1,0:T(8,128)(2,1)}, bf16[512,384]{1,0:T(8,128)(2,1)}, u32[]{:S(2)}, u32[]{:S(2)}) %collective-permute-start.5) | collective-permute-done | bytes 393248 | tf_op jit(solution)/shard_map/ppermute | solution.py:24
  66.1 0.9 collective-permute-start.8
  67.0 7.5 %collective-permute-done.11.refs_7_.refs_0_ = bf16[512,384]{1,0:T(8,128)(2,1)} collective-permute-done((bf16[512,384]{1,0:T(8,128)(2,1)}, bf16[512,384]{1,0:T(8,128)(2,1)}, u32[]{:S(2)}, u32[]{:S(2)}) %collective-permute-start.11) | collective-permute-done | bytes 393248 | tf_op jit(solution)/shard_map/ppermute | solution.py:24
  74.5 4.9 %collective-permute-start.20 = (bf16[3,192,384]{2,1,0:T(8,128)(2,1)}, bf16[3,192,384]{2,1,0:T(8,128)(2,1)S(1)}, u32[]{:S(2)}, u32[]{:S(2)}) collective-permute-start(bf16[3,192,384]{2,1,0:T(8,128)(2,1)} %collective-permute-done.19.refs_0_), channel_id=1, source_target_pairs={{0,4},{4,0},{8,12},{12,8},{16,20},{20,16},{24,28},{28,24},{1,5},{5... | collective-permute-start | bytes 1327112 | tf_op jit(solution)/shard_map/ppermute | solution.py:29
  79.5 1.9 %copy-done.1 = bf16[1536,1024]{1,0:T(8,128)(2,1)S(1)} copy-done((bf16[1536,1024]{1,0:T(8,128)(2,1)S(1)}, bf16[1536,1024]{1,0:T(8,128)(2,1)}, u32[]{:S(2)}) %copy-start.1) | copy-done | bytes 3145752
  81.4 1.3 shard_map.95
  82.8 1.4 collective-permute-done.23.refs_4_
  84.2 2.0 %collective-permute-start.24 = (bf16[3,192,384]{2,1,0:T(8,128)(2,1)}, bf16[3,192,384]{2,1,0:T(8,128)(2,1)S(1)}, u32[]{:S(2)}, u32[]{:S(2)}) collective-permute-start(bf16[3,192,384]{2,1,0:T(8,128)(2,1)} %collective-permute-done.23.refs_4_), channel_id=1, source_target_pairs={{0,4},{4,0},{8,12},{12,8},{16,20},{20,16},{24,28},{28,24},{1,5},{5... | collective-permute-start | bytes 1327112 | tf_op jit(solution)/shard_map/ppermute | solution.py:29
  86.2 7.5 %collective-permute-done.25.refs_6_ = bf16[3,192,384]{2,1,0:T(8,128)(2,1)} collective-permute-done((bf16[3,192,384]{2,1,0:T(8,128)(2,1)}, bf16[3,192,384]{2,1,0:T(8,128)(2,1)}, u32[]{:S(2)}, u32[]{:S(2)}) %collective-permute-start.25) | collective-permute-done | bytes 442400 | tf_op jit(solution)/shard_map/ppermute | solution.py:29
  93.6 1.2 collective-permute-start.26
  95.0 7.1 %shard_map.98 = (bf16[1024,1536]{1,0:T(8,128)(2,1)S(1)}, bf16[16,1536]{1,0:T(8,128)(2,1)S(1)}, bf16[1024,384]{1,0:T(8,128)(2,1)S(1)}) custom-call(s32[2]{0:T(128)S(1)} %add_convert_fusion.ends_ref, bf16[1536,1152]{1,0:T(8,128)(2,1)S(1)} %get-tuple-element.27.w_ref, f32[8,384]{1,0:T(8,128)S(1)} %copy-done.21, f32[8,384]{1,0:T(8,128)S(1)} %copy-done.23, ...), custom_call_target="tpu_custom_call" | custom-call | flops 3623878656 | bytes 6684672 | tf_op jit(solution)/shard_map/pallas_call | solution.py:364
  102.1 1.0 collective-permute-start.29
  103.2 6.7 %shard_map.99 = (bf16[1024,1536]{1,0:T(8,128)(2,1)S(1)}, bf16[512,384]{1,0:T(8,128)(2,1)S(1)}, bf16[512,384]{1,0:T(8,128)(2,1)S(1)}) custom-call(s32[2]{0:T(128)S(1)} %add_convert_fusion.ends_ref, bf16[1536,1152]{1,0:T(8,128)(2,1)S(1)} %get-tuple-element.27.w_ref, f32[8,384]{1,0:T(8,128)S(1)} %copy-done.21, f32[8,384]{1,0:T(8,128)S(1)} %copy-done.23, ...), custom_call_target="tpu_custom_call" | custom-call | flops 3623878656 | bytes 6684672 | tf_op jit(solution)/shard_map/pallas_call | solution.py:364
  109.9 1.3 collective-permute-start.27
  111.2 0.8 collective-permute-start.28
  112.0 0.9 collective-permute-start.17
  112.9 2.3 %shard_map.101.w_ref = bf16[1536,1152]{1,0:T(8,128)(2,1)S(1)} custom-call(s32[2]{0:T(128)S(1)} %pad_add_fusion.t_ref.where_ref, bf16[3,192,384]{2,1,0:T(8,128)(2,1)} %collective-permute-done.19.refs_0_, bf16[3,192,384]{2,1,0:T(8,128)(2,1)S(1)} %collective-permute-done.20.refs_1_, bf16[3,192,384]{2,1,0:T(8,128)(2,1)} %collective-permute-done.21.refs_2_, ...), custom_call_target="tpu_custom_call" | custom-call | bytes 7077888 | tf_op jit(solution)/shard_map/pallas_call | solution.py:298
  115.2 5.4 %shard_map.102.refs_3_ = bf16[1024,384]{1,0:T(8,128)(2,1)S(1)} custom-call(bf16[1536,1152]{1,0:T(8,128)(2,1)S(1)} %shard_map.101.w_ref, bf16[16,1536]{1,0:T(8,128)(2,1)S(1)} %get-tuple-element.35.refs_12_.edge_ref, bf16[1024,1536]{1,0:T(8,128)(2,1)S(1)} %get-tuple-element.37.hidden_ref, bf16[512,384]{1,0:T(8,128)(2,1)} %collective-permute-done.5.refs_7_.refs_0_, ...), custom_call_target="tpu_custom_call" | custom-call | flops 3623878656 | bytes 6684672 | tf_op jit(solution)/shard_map/pallas_call | solution.py:381
  120.7 5.5 %shard_map.103.refs_3_ = bf16[1024,384]{1,0:T(8,128)(2,1)S(1)} custom-call(bf16[1536,1152]{1,0:T(8,128)(2,1)S(1)} %shard_map.101.w_ref, bf16[16,1536]{1,0:T(8,128)(2,1)S(1)} %get-tuple-element.35.refs_12_.edge_ref, bf16[1024,1536]{1,0:T(8,128)(2,1)S(1)} %get-tuple-element.40.hidden_ref, bf16[512,384]{1,0:T(8,128)(2,1)} %collective-permute-done.11.refs_7_.refs_0_, ...), custom_call_target="tpu_custom_call" | custom-call | flops 3623878656 | bytes 6684672 | tf_op jit(solution)/shard_map/pallas_call | solution.py:381
  126.4 5.7 %shard_map.104 = (bf16[4,512,1024]{2,1,0:T(8,128)(2,1)}, f32[32,1024]{1,0:T(8,128)S(1)}, f32[8,1024]{1,0:T(8,128)S(1)}) custom-call(bf16[1536,1024]{1,0:T(8,128)(2,1)S(1)} %get-tuple-element.26.w_ref, f32[1024]{0:T(1024)S(1)} %copy-done.6, s32[4,512]{1,0:T(4,128)S(1)} %copy-done.5, bf16[1024,384]{1,0:T(8,128)(2,1)S(1)} %get-tuple-element.39.refs_0_, ...), custom_call_target="tpu_custom_call" | custom-call | flops 3221225472 | bytes 8388608 | tf_op jit(solution)/shard_map/pallas_call | solution.py:413
  132.1 3.7 %shard_map.105 = (bf16[4,512,1024]{2,1,0:T(8,128)(2,1)}, f32[32,1024]{1,0:T(8,128)S(1)}, f32[8,1024]{1,0:T(8,128)S(1)}) custom-call(bf16[1536,1024]{1,0:T(8,128)(2,1)S(1)} %get-tuple-element.26.w_ref, f32[1024]{0:T(1024)S(1)} %copy-done.6, s32[4,512]{1,0:T(4,128)S(1)} %copy-done.5, ...), custom_call_target="tpu_custom_call", output_to_operand_aliasing={{0}: (9, {})} | custom-call | flops 1610612736 | bytes 5767168 | tf_op jit(solution)/shard_map/pallas_call | solution.py:413
  135.8 2.3 %collective-permute-done.17.refs_1_ = bf16[512,384]{1,0:T(8,128)(2,1)S(1)} collective-permute-done((bf16[512,384]{1,0:T(8,128)(2,1)S(1)}, bf16[512,384]{1,0:T(8,128)(2,1)S(1)}, u32[]{:S(2)}, u32[]{:S(2)}) %collective-permute-start.17) | collective-permute-done | bytes 393248 | tf_op jit(solution)/shard_map/ppermute | solution.py:24
  138.1 0.6 collective-permute-done.18.refs_2_
  138.8 3.7 %shard_map.106 = (bf16[4,512,1024]{2,1,0:T(8,128)(2,1)}, f32[32,1024]{1,0:T(8,128)S(1)}, f32[8,1024]{1,0:T(8,128)S(1)}) custom-call(bf16[1536,1024]{1,0:T(8,128)(2,1)S(1)} %get-tuple-element.26.w_ref, f32[1024]{0:T(1024)S(1)} %copy-done.6, s32[4,512]{1,0:T(4,128)S(1)} %copy-done.5, ...), custom_call_target="tpu_custom_call", output_to_operand_aliasing={{0}: (9, {})} | custom-call | flops 1610612736 | bytes 5767168 | tf_op jit(solution)/shard_map/pallas_call | solution.py:413
  142.4 3.1 %collective-permute-start.31 = (f32[8,1024]{1,0:T(8,128)S(1)}, f32[8,1024]{1,0:T(8,128)S(1)}, u32[]{:S(2)}, u32[]{:S(2)}) collective-permute-start(f32[8,1024]{1,0:T(8,128)S(1)} %get-tuple-element.49), channel_id=1, source_target_pairs={{4,0},{8,4},{12,8},{16,12},{20,16},{24,20},{28,24},{5,1},{9,5},{13... | collective-permute-start | bytes 98312 | tf_op jit(solution)/shard_map/ppermute | solution.py:39
  145.6 1.9 %collective-permute-start.32 = (f32[8,128]{1,0:T(8,128)S(1)}, f32[8,128]{1,0:T(8,128)S(1)}, u32[]{:S(2)}, u32[]{:S(2)}) collective-permute-start(f32[8,128]{1,0:T(8,128)S(1)} %slice.4), channel_id=1, source_target_pairs={{4,0},{8,4},{12,8},{16,12},{20,16},{24,20},{28,24},{5,1},{9,5},{13... | collective-permute-start | bytes 12296 | tf_op jit(solution)/shard_map/ppermute | solution.py:39
  147.6 3.0 %collective-permute-done.32.got_count_ref = f32[8,128]{1,0:T(8,128)S(1)} collective-permute-done((f32[8,128]{1,0:T(8,128)S(1)}, f32[8,128]{1,0:T(8,128)S(1)}, u32[]{:S(2)}, u32[]{:S(2)}) %collective-permute-start.32) | collective-permute-done | bytes 4128 | tf_op jit(solution)/shard_map/ppermute | solution.py:39
  150.6 1.3 shard_map.108
  (75 shorter events, 0.7 us)
Async XLA Ops:
  0.6 78.8 %copy-start = (bf16[3,1536,384]{2,1,0:T(8,128)(2,1)S(1)}, bf16[3,1536,384]{2,1,0:T(8,128)(2,1)}, u32[]{:S(2)}) copy-start(bf16[3,1536,384]{2,1,0:T(8,128)(2,1)} %w_ref.3) | copy-start | bytes 10616836
  2.6 34.2 %collective-permute-start.19 = (bf16[3,192,384]{2,1,0:T(8,128)(2,1)}, bf16[3,192,384]{2,1,0:T(8,128)(2,1)}, u32[]{:S(2)}, u32[]{:S(2)}) collective-permute-start(bf16[3,192,384]{2,1,0:T(8,128)(2,1)} %shard_map.100), channel_id=1, source_target_pairs={{0,3},{1,2},{2,1},{3,0},{4,7},{5,6},{6,5},{7,4},{8,11},{9,10},{10,... | collective-permute-start | bytes 1327112 | tf_op jit(solution)/shard_map/ppermute | solution.py:24
  8.4 26.2 %collective-permute-start.3 = (bf16[512,384]{1,0:T(8,128)(2,1)}, bf16[512,384]{1,0:T(8,128)(2,1)}, u32[]{:S(2)}, u32[]{:S(2)}) collective-permute-start(bf16[512,384]{1,0:T(8,128)(2,1)} %get-tuple-element.29.refs_4_), channel_id=1, source_target_pairs={{0,1},{1,0},{2,3},{3,2},{4,5},{5,4},{6,7},{7,6},{8,9},{9,8},{10,11... | collective-permute-start | bytes 1179656 | tf_op jit(solution)/shard_map/ppermute | solution.py:24
  8.7 27.1 %collective-permute-start.4 = (bf16[512,384]{1,0:T(8,128)(2,1)}, bf16[512,384]{1,0:T(8,128)(2,1)S(1)}, u32[]{:S(2)}, u32[]{:S(2)}) collective-permute-start(bf16[512,384]{1,0:T(8,128)(2,1)} %get-tuple-element.29.refs_4_), channel_id=1, source_target_pairs={{0,2},{1,3},{2,0},{3,1},{4,6},{5,7},{6,4},{7,5},{8,10},{9,11},{10,... | collective-permute-start | bytes 1179656 | tf_op jit(solution)/shard_map/ppermute | solution.py:24
  8.8 6.7 %collective-permute-start.12 = (bf16[8,384]{1,0:T(8,128)(2,1)}, bf16[8,384]{1,0:T(8,128)(2,1)S(1)}, u32[]{:S(2)}, u32[]{:S(2)}) collective-permute-start(bf16[8,384]{1,0:T(8,128)(2,1)} %get-tuple-element.33), channel_id=1, source_target_pairs={{0,4},{4,8},{8,12},{12,16},{16,20},{20,24},{24,28},{1,5},{5,9},{9,... | collective-permute-start | bytes 18440 | tf_op jit(solution)/shard_map/ppermute | solution.py:39
  13.5 5.6 %collective-permute-start.13 = (bf16[8,384]{1,0:T(8,128)(2,1)}, bf16[8,384]{1,0:T(8,128)(2,1)S(1)}, u32[]{:S(2)}, u32[]{:S(2)}) collective-permute-start(bf16[8,384]{1,0:T(8,128)(2,1)} %get-tuple-element.34), channel_id=1, source_target_pairs={{4,0},{8,4},{12,8},{16,12},{20,16},{24,20},{28,24},{5,1},{9,5},{13... | collective-permute-start | bytes 18440 | tf_op jit(solution)/shard_map/ppermute | solution.py:39
  15.5 9.0 %collective-permute-start = (f32[8,384]{1,0:T(8,128)}, f32[8,384]{1,0:T(8,128)S(1)}, u32[]{:S(2)}, u32[]{:S(2)}) collective-permute-start(f32[8,384]{1,0:T(8,128)} %get-tuple-element.28.refs_0_), channel_id=1, source_target_pairs={{0,1},{1,0},{2,3},{3,2},{4,5},{5,4},{6,7},{7,6},{8,9},{9,8},{10,11... | collective-permute-start | bytes 36872 | tf_op jit(solution)/shard_map/ppermute | solution.py:24
  19.1 20.0 %collective-permute-start.6 = (bf16[512,384]{1,0:T(8,128)(2,1)}, bf16[512,384]{1,0:T(8,128)(2,1)S(1)}, u32[]{:S(2)}, u32[]{:S(2)}) collective-permute-start(bf16[512,384]{1,0:T(8,128)(2,1)} %get-tuple-element.30.refs_8_), channel_id=1, source_target_pairs={{0,1},{1,0},{2,3},{3,2},{4,5},{5,4},{6,7},{7,6},{8,9},{9,8},{10,11... | collective-permute-start | bytes 1179656 | tf_op jit(solution)/shard_map/ppermute | solution.py:24
  24.5 0.6 copy-start.22
  25.1 3.1 %collective-permute-start.1 = (f32[8,384]{1,0:T(8,128)}, f32[8,384]{1,0:T(8,128)S(1)}, u32[]{:S(2)}, u32[]{:S(2)}) collective-permute-start(f32[8,384]{1,0:T(8,128)} %get-tuple-element.28.refs_0_), channel_id=1, source_target_pairs={{0,2},{1,3},{2,0},{3,1},{4,6},{5,7},{6,4},{7,5},{8,10},{9,11},{10,... | collective-permute-start | bytes 36872 | tf_op jit(solution)/shard_map/ppermute | solution.py:24
  28.2 0.6 copy-start.24
  28.8 4.1 %collective-permute-start.2 = (f32[8,384]{1,0:T(8,128)}, f32[8,384]{1,0:T(8,128)S(1)}, u32[]{:S(2)}, u32[]{:S(2)}) collective-permute-start(f32[8,384]{1,0:T(8,128)} %get-tuple-element.28.refs_0_), channel_id=1, source_target_pairs={{0,3},{1,2},{2,1},{3,0},{4,7},{5,6},{6,5},{7,4},{8,11},{9,10},{10,... | collective-permute-start | bytes 36872 | tf_op jit(solution)/shard_map/ppermute | solution.py:24
  32.9 0.6 copy-start.26
  33.4 7.1 %collective-permute-start.7 = (bf16[512,384]{1,0:T(8,128)(2,1)}, bf16[512,384]{1,0:T(8,128)(2,1)S(1)}, u32[]{:S(2)}, u32[]{:S(2)}) collective-permute-start(bf16[512,384]{1,0:T(8,128)(2,1)} %get-tuple-element.30.refs_8_), channel_id=1, source_target_pairs={{0,2},{1,3},{2,0},{3,1},{4,6},{5,7},{6,4},{7,5},{8,10},{9,11},{10,... | collective-permute-start | bytes 1179656 | tf_op jit(solution)/shard_map/ppermute | solution.py:24
  34.6 8.8 %collective-permute-start.9 = (bf16[512,384]{1,0:T(8,128)(2,1)}, bf16[512,384]{1,0:T(8,128)(2,1)}, u32[]{:S(2)}, u32[]{:S(2)}) collective-permute-start(bf16[512,384]{1,0:T(8,128)(2,1)} %get-tuple-element.31.refs_4_), channel_id=1, source_target_pairs={{0,1},{1,0},{2,3},{3,2},{4,5},{5,4},{6,7},{7,6},{8,9},{9,8},{10,11... | collective-permute-start | bytes 1179656 | tf_op jit(solution)/shard_map/ppermute | solution.py:24
  35.8 0.8 copy-start.12
  36.6 12.4 %collective-permute-start.10 = (bf16[512,384]{1,0:T(8,128)(2,1)}, bf16[512,384]{1,0:T(8,128)(2,1)S(1)}, u32[]{:S(2)}, u32[]{:S(2)}) collective-permute-start(bf16[512,384]{1,0:T(8,128)(2,1)} %get-tuple-element.31.refs_4_), channel_id=1, source_target_pairs={{0,2},{1,3},{2,0},{3,1},{4,6},{5,7},{6,4},{7,5},{8,10},{9,11},{10,... | collective-permute-start | bytes 1179656 | tf_op jit(solution)/shard_map/ppermute | solution.py:24
  36.8 17.7 %collective-permute-start.21 = (bf16[3,192,384]{2,1,0:T(8,128)(2,1)}, bf16[3,192,384]{2,1,0:T(8,128)(2,1)}, u32[]{:S(2)}, u32[]{:S(2)}) collective-permute-start(bf16[3,192,384]{2,1,0:T(8,128)(2,1)} %collective-permute-done.19.refs_0_), channel_id=1, source_target_pairs={{0,8},{4,12},{8,0},{12,4},{16,24},{20,28},{24,16},{28,20},{1,9},{5... | collective-permute-start | bytes 1327112 | tf_op jit(solution)/shard_map/ppermute | solution.py:29
  38.1 1.0 copy-start.2
  39.1 55.7 %copy-start.21 = (f32[8,384]{1,0:T(8,128)S(1)}, f32[8,384]{1,0:T(8,128)}, u32[]{:S(2)}) copy-start(f32[8,384]{1,0:T(8,128)} %get-tuple-element.28.refs_0_) | copy-start | bytes 36868
  39.2 0.8 copy-start.15
  39.9 11.9 %collective-permute-start.14 = (bf16[528,384]{1,0:T(8,128)(2,1)S(1)}, bf16[528,384]{1,0:T(8,128)(2,1)S(1)}, u32[]{:S(2)}, u32[]{:S(2)}) collective-permute-start(bf16[528,384]{1,0:T(8,128)(2,1)S(1)} %shard_map.97.refs_8_), channel_id=1, source_target_pairs={{0,1},{1,0},{2,3},{3,2},{4,5},{5,4},{6,7},{7,6},{8,9},{9,8},{10,11... | collective-permute-start | bytes 1216520 | tf_op jit(solution)/shard_map/ppermute | solution.py:24
  40.6 17.0 %copy-start.17 = (bf16[512,384]{1,0:T(8,128)(2,1)}, bf16[512,384]{1,0:T(8,128)(2,1)S(1)}, u32[]{:S(2)}) copy-start(bf16[512,384]{1,0:T(8,128)(2,1)S(1)} %collective-permute-done.7.refs_10_) | copy-start | bytes 1179652
  40.6 17.0 %collective-permute-start.15 = (bf16[528,384]{1,0:T(8,128)(2,1)S(1)}, bf16[528,384]{1,0:T(8,128)(2,1)}, u32[]{:S(2)}, u32[]{:S(2)}) collective-permute-start(bf16[528,384]{1,0:T(8,128)(2,1)S(1)} %shard_map.97.refs_8_), channel_id=1, source_target_pairs={{0,2},{1,3},{2,0},{3,1},{4,6},{5,7},{6,4},{7,5},{8,10},{9,11},{10,... | collective-permute-start | bytes 1216520 | tf_op jit(solution)/shard_map/ppermute | solution.py:24
  42.6 0.7 copy-start.3
  43.4 22.7 %collective-permute-start.5 = (bf16[512,384]{1,0:T(8,128)(2,1)}, bf16[512,384]{1,0:T(8,128)(2,1)}, u32[]{:S(2)}, u32[]{:S(2)}) collective-permute-start(bf16[512,384]{1,0:T(8,128)(2,1)} %collective-permute-done.3.refs_5_), channel_id=1, source_target_pairs={{0,2},{1,3},{2,0},{3,1},{4,6},{5,7},{6,4},{7,5},{8,10},{9,11},{10,... | collective-permute-start | bytes 1179656 | tf_op jit(solution)/shard_map/ppermute | solution.py:24
  49.0 0.8 copy-start.19
  49.8 24.8 %collective-permute-start.11 = (bf16[512,384]{1,0:T(8,128)(2,1)}, bf16[512,384]{1,0:T(8,128)(2,1)}, u32[]{:S(2)}, u32[]{:S(2)}) collective-permute-start(bf16[512,384]{1,0:T(8,128)(2,1)} %collective-permute-done.9.refs_5_), channel_id=1, source_target_pairs={{0,2},{1,3},{2,0},{3,1},{4,6},{5,7},{6,4},{7,5},{8,10},{9,11},{10,... | collective-permute-start | bytes 1179656 | tf_op jit(solution)/shard_map/ppermute | solution.py:24
  51.9 0.8 copy-start.8
  52.6 31.5 %collective-permute-start.23 = (bf16[3,192,384]{2,1,0:T(8,128)(2,1)}, bf16[3,192,384]{2,1,0:T(8,128)(2,1)}, u32[]{:S(2)}, u32[]{:S(2)}) collective-permute-start(bf16[3,192,384]{2,1,0:T(8,128)(2,1)} %collective-permute-done.19.refs_0_), channel_id=1, source_target_pairs={{0,16},{4,20},{8,24},{12,28},{16,0},{20,4},{24,8},{28,12},{1,17},{... | collective-permute-start | bytes 1327112 | tf_op jit(solution)/shard_map/ppermute | solution.py:29
  54.5 39.1 %collective-permute-start.25 = (bf16[3,192,384]{2,1,0:T(8,128)(2,1)}, bf16[3,192,384]{2,1,0:T(8,128)(2,1)}, u32[]{:S(2)}, u32[]{:S(2)}) collective-permute-start(bf16[3,192,384]{2,1,0:T(8,128)(2,1)} %collective-permute-done.21.refs_2_), channel_id=1, source_target_pairs={{0,16},{4,20},{8,24},{12,28},{16,0},{20,4},{24,8},{28,12},{1,17},{... | collective-permute-start | bytes 1327112 | tf_op jit(solution)/shard_map/ppermute | solution.py:29
  57.6 25.2 %collective-permute-start.16 = (bf16[528,384]{1,0:T(8,128)(2,1)}, bf16[528,384]{1,0:T(8,128)(2,1)}, u32[]{:S(2)}, u32[]{:S(2)}) collective-permute-start(bf16[528,384]{1,0:T(8,128)(2,1)} %collective-permute-done.15.refs_10_), channel_id=1, source_target_pairs={{0,1},{1,0},{2,3},{3,2},{4,5},{5,4},{6,7},{7,6},{8,9},{9,8},{10,11... | collective-permute-start | bytes 1216520 | tf_op jit(solution)/shard_map/ppermute | solution.py:24
  66.1 36.0 %collective-permute-start.8 = (bf16[512,384]{1,0:T(8,128)(2,1)}, bf16[512,384]{1,0:T(8,128)(2,1)S(1)}, u32[]{:S(2)}, u32[]{:S(2)}) collective-permute-start(bf16[512,384]{1,0:T(8,128)(2,1)} %copy-done.17), channel_id=1, source_target_pairs={{0,1},{1,0},{2,3},{3,2},{4,5},{5,4},{6,7},{7,6},{8,9},{9,8},{10,11... | collective-permute-start | bytes 1179656 | tf_op jit(solution)/shard_map/ppermute | solution.py:24
  74.5 28.6 %collective-permute-start.20 = (bf16[3,192,384]{2,1,0:T(8,128)(2,1)}, bf16[3,192,384]{2,1,0:T(8,128)(2,1)S(1)}, u32[]{:S(2)}, u32[]{:S(2)}) collective-permute-start(bf16[3,192,384]{2,1,0:T(8,128)(2,1)} %collective-permute-done.19.refs_0_), channel_id=1, source_target_pairs={{0,4},{4,0},{8,12},{12,8},{16,20},{20,16},{24,28},{28,24},{1,5},{5... | collective-permute-start | bytes 1327112 | tf_op jit(solution)/shard_map/ppermute | solution.py:29
  79.5 1.9 %copy-start.1 = (bf16[1536,1024]{1,0:T(8,128)(2,1)S(1)}, bf16[1536,1024]{1,0:T(8,128)(2,1)}, u32[]{:S(2)}) copy-start(bf16[1536,1024]{1,0:T(8,128)(2,1)} %head_ref.1) | copy-start | bytes 9437188
  81.4 13.5 %copy-start.4 = (bf16[528,384]{1,0:T(8,128)(2,1)S(1)}, bf16[528,384]{1,0:T(8,128)(2,1)}, u32[]{:S(2)}) copy-start(bf16[528,384]{1,0:T(8,128)(2,1)} %copy-done.3) | copy-start | bytes 1216516
  81.4 13.5 %copy-start.9 = (bf16[528,384]{1,0:T(8,128)(2,1)S(1)}, bf16[528,384]{1,0:T(8,128)(2,1)}, u32[]{:S(2)}) copy-start(bf16[528,384]{1,0:T(8,128)(2,1)} %copy-done.8) | copy-start | bytes 1216516
  81.4 13.5 %copy-start.14 = (bf16[512,384]{1,0:T(8,128)(2,1)S(1)}, bf16[512,384]{1,0:T(8,128)(2,1)}, u32[]{:S(2)}) copy-start(bf16[512,384]{1,0:T(8,128)(2,1)} %get-tuple-element.31.refs_4_) | copy-start | bytes 1179652
  81.4 13.5 %copy-start.20 = (bf16[512,384]{1,0:T(8,128)(2,1)S(1)}, bf16[512,384]{1,0:T(8,128)(2,1)}, u32[]{:S(2)}) copy-start(bf16[512,384]{1,0:T(8,128)(2,1)} %copy-done.19) | copy-start | bytes 1179652
  81.4 13.5 %copy-start.23 = (f32[8,384]{1,0:T(8,128)S(1)}, f32[8,384]{1,0:T(8,128)}, u32[]{:S(2)}) copy-start(f32[8,384]{1,0:T(8,128)} %copy-done.22) | copy-start | bytes 36868
  81.4 13.5 %copy-start.25 = (f32[8,384]{1,0:T(8,128)S(1)}, f32[8,384]{1,0:T(8,128)}, u32[]{:S(2)}) copy-start(f32[8,384]{1,0:T(8,128)} %copy-done.24) | copy-start | bytes 36868
  81.4 13.5 %copy-start.27 = (f32[8,384]{1,0:T(8,128)S(1)}, f32[8,384]{1,0:T(8,128)}, u32[]{:S(2)}) copy-start(f32[8,384]{1,0:T(8,128)} %copy-done.26) | copy-start | bytes 36868
  82.7 27.2 %collective-permute-start.22 = (bf16[3,192,384]{2,1,0:T(8,128)(2,1)}, bf16[3,192,384]{2,1,0:T(8,128)(2,1)S(1)}, u32[]{:S(2)}, u32[]{:S(2)}) collective-permute-start(bf16[3,192,384]{2,1,0:T(8,128)(2,1)} %collective-permute-done.21.refs_2_), channel_id=1, source_target_pairs={{0,4},{4,0},{8,12},{12,8},{16,20},{20,16},{24,28},{28,24},{1,5},{5... | collective-permute-start | bytes 1327112 | tf_op jit(solution)/shard_map/ppermute | solution.py:29
  84.2 27.0 %collective-permute-start.24 = (bf16[3,192,384]{2,1,0:T(8,128)(2,1)}, bf16[3,192,384]{2,1,0:T(8,128)(2,1)S(1)}, u32[]{:S(2)}, u32[]{:S(2)}) collective-permute-start(bf16[3,192,384]{2,1,0:T(8,128)(2,1)} %collective-permute-done.23.refs_4_), channel_id=1, source_target_pairs={{0,4},{4,0},{8,12},{12,8},{16,20},{20,16},{24,28},{28,24},{1,5},{5... | collective-permute-start | bytes 1327112 | tf_op jit(solution)/shard_map/ppermute | solution.py:29
  93.6 18.3 %collective-permute-start.26 = (bf16[3,192,384]{2,1,0:T(8,128)(2,1)}, bf16[3,192,384]{2,1,0:T(8,128)(2,1)S(1)}, u32[]{:S(2)}, u32[]{:S(2)}) collective-permute-start(bf16[3,192,384]{2,1,0:T(8,128)(2,1)} %collective-permute-done.25.refs_6_), channel_id=1, source_target_pairs={{0,4},{4,0},{8,12},{12,8},{16,20},{20,16},{24,28},{28,24},{1,5},{5... | collective-permute-start | bytes 1327112 | tf_op jit(solution)/shard_map/ppermute | solution.py:29
  94.9 8.2 %copy-start.10 = (bf16[512,384]{1,0:T(8,128)(2,1)S(1)}, bf16[512,384]{1,0:T(8,128)(2,1)}, u32[]{:S(2)}) copy-start(bf16[512,384]{1,0:T(8,128)(2,1)} %get-tuple-element.29.refs_4_) | copy-start | bytes 1179652
  94.9 8.2 %copy-start.11 = (bf16[512,384]{1,0:T(8,128)(2,1)S(1)}, bf16[512,384]{1,0:T(8,128)(2,1)}, u32[]{:S(2)}) copy-start(bf16[512,384]{1,0:T(8,128)(2,1)} %get-tuple-element.30.refs_8_) | copy-start | bytes 1179652
  94.9 8.2 %copy-start.13 = (bf16[512,384]{1,0:T(8,128)(2,1)S(1)}, bf16[512,384]{1,0:T(8,128)(2,1)}, u32[]{:S(2)}) copy-start(bf16[512,384]{1,0:T(8,128)(2,1)} %copy-done.12) | copy-start | bytes 1179652
  94.9 8.2 %copy-start.16 = (bf16[512,384]{1,0:T(8,128)(2,1)S(1)}, bf16[512,384]{1,0:T(8,128)(2,1)}, u32[]{:S(2)}) copy-start(bf16[512,384]{1,0:T(8,128)(2,1)} %copy-done.15) | copy-start | bytes 1179652
  95.0 8.2 %copy-start.18 = (bf16[512,384]{1,0:T(8,128)(2,1)S(1)}, bf16[512,384]{1,0:T(8,128)(2,1)}, u32[]{:S(2)}) copy-start(bf16[512,384]{1,0:T(8,128)(2,1)} %copy-done.17) | copy-start | bytes 1179652
  102.1 24.1 %collective-permute-start.29 = (bf16[1024,384]{1,0:T(8,128)(2,1)S(1)}, bf16[1024,384]{1,0:T(8,128)(2,1)S(1)}, u32[]{:S(2)}, u32[]{:S(2)}) collective-permute-start(bf16[1024,384]{1,0:T(8,128)(2,1)S(1)} %get-tuple-element.39.refs_0_), channel_id=1, source_target_pairs={{0,1},{1,0},{2,3},{3,2},{4,5},{5,4},{6,7},{7,6},{8,9},{9,8},{10,11... | collective-permute-start | bytes 2359304 | tf_op jit(solution)/shard_map/ppermute | solution.py:24
  103.1 23.3 %collective-permute-start.30 = (bf16[1024,384]{1,0:T(8,128)(2,1)S(1)}, bf16[1024,384]{1,0:T(8,128)(2,1)S(1)}, u32[]{:S(2)}, u32[]{:S(2)}) collective-permute-start(bf16[1024,384]{1,0:T(8,128)(2,1)S(1)} %get-tuple-element.39.refs_0_), channel_id=1, source_target_pairs={{0,2},{1,3},{2,0},{3,1},{4,6},{5,7},{6,4},{7,5},{8,10},{9,11},{10,... | collective-permute-start | bytes 2359304 | tf_op jit(solution)/shard_map/ppermute | solution.py:24
  109.9 22.2 %collective-permute-start.27 = (bf16[512,384]{1,0:T(8,128)(2,1)S(1)}, bf16[512,384]{1,0:T(8,128)(2,1)S(1)}, u32[]{:S(2)}, u32[]{:S(2)}) collective-permute-start(bf16[512,384]{1,0:T(8,128)(2,1)S(1)} %get-tuple-element.38.refs_0_), channel_id=1, source_target_pairs={{0,1},{1,0},{2,3},{3,2},{4,5},{5,4},{6,7},{7,6},{8,9},{9,8},{10,11... | collective-permute-start | bytes 1179656 | tf_op jit(solution)/shard_map/ppermute | solution.py:24
  111.2 20.9 %collective-permute-start.28 = (bf16[512,384]{1,0:T(8,128)(2,1)S(1)}, bf16[512,384]{1,0:T(8,128)(2,1)S(1)}, u32[]{:S(2)}, u32[]{:S(2)}) collective-permute-start(bf16[512,384]{1,0:T(8,128)(2,1)S(1)} %get-tuple-element.38.refs_0_), channel_id=1, source_target_pairs={{0,2},{1,3},{2,0},{3,1},{4,6},{5,7},{6,4},{7,5},{8,10},{9,11},{10,... | collective-permute-start | bytes 1179656 | tf_op jit(solution)/shard_map/ppermute | solution.py:24
  112.0 26.1 %collective-permute-start.17 = (bf16[512,384]{1,0:T(8,128)(2,1)S(1)}, bf16[512,384]{1,0:T(8,128)(2,1)S(1)}, u32[]{:S(2)}, u32[]{:S(2)}) collective-permute-start(bf16[512,384]{1,0:T(8,128)(2,1)S(1)} %get-tuple-element.36.refs_0_), channel_id=1, source_target_pairs={{0,1},{1,0},{2,3},{3,2},{4,5},{5,4},{6,7},{7,6},{8,9},{9,8},{10,11... | collective-permute-start | bytes 1179656 | tf_op jit(solution)/shard_map/ppermute | solution.py:24
  120.6 5.7 %copy-start.5 = (s32[4,512]{1,0:T(4,128)S(1)}, s32[4,512]{1,0:T(4,128)}, u32[]{:S(2)}) copy-start(s32[4,512]{1,0:T(4,128)} %slot_ref.7) | copy-start | bytes 24580
  120.7 5.7 %copy-start.6 = (f32[1024]{0:T(1024)S(1)}, f32[1024]{0:T(1024)}, u32[]{:S(2)}) copy-start(f32[1024]{0:T(1024)} %bias_ref.7) | copy-start | bytes 12292
  126.2 12.5 %collective-permute-start.18 = (bf16[512,384]{1,0:T(8,128)(2,1)S(1)}, bf16[512,384]{1,0:T(8,128)(2,1)S(1)}, u32[]{:S(2)}, u32[]{:S(2)}) collective-permute-start(bf16[512,384]{1,0:T(8,128)(2,1)S(1)} %get-tuple-element.36.refs_0_), channel_id=1, source_target_pairs={{0,2},{1,3},{2,0},{3,1},{4,6},{5,7},{6,4},{7,5},{8,10},{9,11},{10,... | collective-permute-start | bytes 1179656 | tf_op jit(solution)/shard_map/ppermute | solution.py:24
  138.7 11.8 %copy-start.7 = (s32[4]{0:T(128)S(1)}, s32[4]{0:T(128)}, u32[]{:S(2)}) copy-start(s32[4]{0:T(128)} %map_ref.1) | copy-start | bytes 52
  142.4 8.1 %collective-permute-start.31 = (f32[8,1024]{1,0:T(8,128)S(1)}, f32[8,1024]{1,0:T(8,128)S(1)}, u32[]{:S(2)}, u32[]{:S(2)}) collective-permute-start(f32[8,1024]{1,0:T(8,128)S(1)} %get-tuple-element.49), channel_id=1, source_target_pairs={{4,0},{8,4},{12,8},{16,12},{20,16},{24,20},{28,24},{5,1},{9,5},{13... | collective-permute-start | bytes 98312 | tf_op jit(solution)/shard_map/ppermute | solution.py:39
  145.6 4.9 %collective-permute-start.32 = (f32[8,128]{1,0:T(8,128)S(1)}, f32[8,128]{1,0:T(8,128)S(1)}, u32[]{:S(2)}, u32[]{:S(2)}) collective-permute-start(f32[8,128]{1,0:T(8,128)S(1)} %slice.4), channel_id=1, source_target_pairs={{4,0},{8,4},{12,8},{16,12},{20,16},{24,20},{28,24},{5,1},{9,5},{13... | collective-permute-start | bytes 12296 | tf_op jit(solution)/shard_map/ppermute | solution.py:39
